TPU v7x, 128 devices: a whole 4x4x4 slice. The times are simulated.
128 devices in a mesh: gx: 16 (over z, x_lo, core), gy: 8 (over x_hi, y).
Axes of the slice: x: 4 (x_hi: 2, x_lo: 2; x = x_hi * 2 + x_lo), y: 4, z: 4, core: 2. Of those that a mesh axis runs over, the one named last changes fastest.
Arguments:
- populations: float32 [19, 64, 256, 128], P(None, 'gx', 'gy'), may hold values from 0.5 to 1.5
- solid: int32 [64, 256, 128], P('gx', 'gy'), may hold values 0 or 1
- panel_cell: int32 [32768], P(('gx', 'gy')), may hold values from 0 to 16383
- panel_owner: int32 [32768], P(('gx', 'gy')), may hold values from 0 to 15, as said below
- panel_count: int32 [128], P(('gx', 'gy')), may hold values from 1 to 256, 16384 in all
- panel_area: float32 [3, 32768], P(None, ('gx', 'gy')), may hold values from -4 to 4
- observers: float32 [3, 256], replicated, may hold values from 0 to 288, as said below
- frequencies: float32 [64], replicated, may hold values from 0.01 to 1.5
Outputs:
- populations_out: float32 [19, 64, 256, 128], P(None, 'gx', 'gy')
- patch_spectra: float32 [16, 2, 64, 256], P('gx', None, 'gy')
Inputs may be any that keep to these rules, and one draw needn't show every extreme that they name: `panel_owner`: among the 256 slots of each brick every patch is named by exactly 16 slots. `panel_count`: the counts of all bricks sum to 16384 and some brick has all 256 slots live. `observers`: every observer lies 16 or more cells above the lattice: its third coordinate is at least 144.
All inputs are finite; a program needn't handle non-finite values. No bound on the sum of `solid` on one device may be relied on, other than what follows from the above.
Results may differ from a plain program's by a relative error of at most 0.0003.
Values sent between devices are 32-bit elements; how exact they have to be, the bound alone decides.
No kernel may reach another device: no remote copies, remote signals or barrier semaphores. Data moves between devices by JAX's collectives and lax.ppermute only.
A program may use at most 64 MiB of HBM per device.

v0:
```python
import functools
import math

import jax
import jax.numpy as jnp
import numpy as np
from jax import lax
from jax.experimental import pallas as pl
from jax.experimental.pallas import tpu as pltpu
from jax.sharding import PartitionSpec as P

F32 = jnp.float32
BF16 = jnp.bfloat16

VEL = [
    (0, 0, 0), (1, 0, 0), (-1, 0, 0), (0, 1, 0), (0, -1, 0), (0, 0, 1), (0, 0, -1),
    (1, 1, 0), (-1, -1, 0), (1, -1, 0), (-1, 1, 0), (1, 0, 1), (-1, 0, -1),
    (1, 0, -1), (-1, 0, 1), (0, 1, 1), (0, -1, -1), (0, 1, -1), (0, -1, 1),
]
NQ = 19
BX, BY, BZ = 4, 32, 128
SOLID = 19
HX = 3
Y0 = 12
YR = 56
SLOTS = 256
PATCH = 16
CAP = 16
NB = 128
NV = 16
BASE = 19.0
VMEM_LIMIT = 60 * 1024 * 1024


def x_entries(side):
    out = []
    for dist in (1, 2, 3):
        for pop in range(NQ):
            along = VEL[pop][0] * side
            if dist == 1 or (dist == 2 and along >= 0) or (dist == 3 and along > 0):
                out.append((pop, dist))
        if dist < 3:
            out.append((SOLID, dist))
    return out


X_UP = x_entries(1)
X_DOWN = x_entries(-1)
NXE = len(X_UP)


def y_entries(side):
    out, at = [], 0
    for x in range(-HX, BX + HX):
        far = -x if x < 0 else (x - BX + 1 if x >= BX else 0)
        inward = 1 if x < 0 else -1
        for pop in range(NQ + 1):
            if pop == SOLID:
                if far > 2:
                    continue
                rows = 3
            else:
                along = VEL[pop][0] * inward
                if (far == 2 and along < 0) or (far == 3 and along <= 0):
                    continue
                rows = 3 + VEL[pop][1] * side
            out.append((pop, x, rows, at))
            at += rows
    return out, at


Y_UP, NYE = y_entries(1)
Y_DOWN, NYE_DOWN = y_entries(-1)
assert NYE == NYE_DOWN


def collide(f, solid):
    pair = [f[i] + f[i + 1] for i in range(1, NQ, 2)]
    diff = [f[i] - f[i + 1] for i in range(1, NQ, 2)]
    px, py, pz, pa, pb, pc, pd, pe, pf = pair
    dx, dy, dz, da, db, dc, dd, de, df = diff
    sxy, sxz, syz = pa + pb, pc + pd, pe + pf
    qxy, qxz, qyz = pa - pb, pc - pd, pe - pf
    rho = (f[0] + px) + (py + pz) + (sxy + (sxz + syz))
    jx = dx + (da + db) + (dc + dd)
    jy = dy + (da - db) + (de + df)
    jz = dz + (dc - dd) + (de - df)
    inv = 1.0 / rho
    ux, uy, uz = jx * inv, jy * inv, jz * inv
    exx, eyy, ezz = jx * ux, jy * uy, jz * uz
    exy, exz, eyz = jx * uy, jx * uz, jy * uz
    base = rho - 1.5 * (exx + eyy + ezz)
    third = rho * (1.0 / 3.0)
    bx = (px + sxy + sxz) - third - exx
    by = (py + sxy + syz) - third - eyy
    bz = (pz + sxz + syz) - third - ezz
    trace = bx + by + bz
    out = [None] * NQ
    out[0] = -0.2 * f[0] + 0.4 * base + trace * (1.0 / 7.0)
    axis_common = base * (0.6 / 9.0) + trace * (0.6 / 7.0)
    diag_common = base * (0.6 / 18.0) + trace * (0.2 / 7.0)
    ax = [0.3 * e - 0.1 * b for e, b in ((exx, bx), (eyy, by), (ezz, bz))]
    dg = [0.15 * e - 0.1 * b for e, b in ((exx, bx), (eyy, by), (ezz, bz))]
    half = [axis_common + a - 0.1 * p for a, p in zip(ax, (px, py, pz))]
    for (i, k), e, q, (p1, p2) in (
        ((0, 1), exy, qxy, (pa, pb)),
        ((0, 2), exz, qxz, (pc, pd)),
        ((1, 2), eyz, qyz, (pe, pf)),
    ):
        common = diag_common + (dg[i] + dg[k])
        twist = 0.3 * e - 0.15 * (q - e)
        half.append(common + twist - 0.1 * p1)
        half.append(common - twist - 0.1 * p2)
    a, b = 0.7 / 3.0, 0.7 / 6.0
    flow = [jx * a, jy * a, jz * a]
    kx, ky, kz = jx * b, jy * b, jz * b
    flow += [kx + ky, kx - ky, kx + kz, kx - kz, ky + kz, ky - kz]
    for n in range(9):
        odd = flow[n] - 0.2 * diff[n]
        out[2 * n + 1] = half[n] + odd
        out[2 * n + 2] = half[n] - odd
    opposite = [0] + [i + 1 if i % 2 else i - 1 for i in range(1, NQ)]
    out = [jnp.where(solid, f[opposite[i]], out[i]) for i in range(NQ)]
    return out, rho, jx, jy, jz


def split3(v):
    hi = v.astype(BF16)
    rest = v - hi.astype(F32)
    mid = rest.astype(BF16)
    lo = (rest - mid.astype(F32)).astype(BF16)
    return hi, mid, lo


def dot(a, b):
    return jnp.dot(a, b, preferred_element_type=F32)


def sample(moments, table, column, rows):
    row_hot = (
        lax.broadcasted_iota(jnp.int32, (SLOTS, rows), 1).astype(F32) == table[:, column : column + 1]
    ).astype(F32).astype(BF16)
    lane = lax.broadcasted_iota(jnp.int32, (SLOTS, BZ), 1).astype(F32)
    z_hot = lane == table[:, 2:3]
    columns = []
    for q in range(4):
        hi, mid, lo = split3(moments[q])
        got = dot(row_hot, hi) + dot(row_hot, mid) + dot(row_hot, lo)
        columns.append(jnp.sum(jnp.where(z_hot, got, 0.0), axis=1, keepdims=True))
    return columns


def put_message(values, out_ref):
    for part in range(2):
        total = jnp.zeros((PATCH, 128), F32)
        for r in range(8):
            at = (part * 8 + r) * PATCH
            block = values[at : at + PATCH, :]
            total = total + (pltpu.roll(block, r * NV, axis=1) if r else block)
        for p in range(PATCH):
            out_ref[p * 8 : p * 8 + 8, part * 128 : part * 128 + 128] = jnp.broadcast_to(
                total[p : p + 1, :], (8, 128)
            )


def lanes_of(columns, start=0):
    lane = lax.broadcasted_iota(jnp.int32, (SLOTS, 128), 1)
    out = jnp.zeros((SLOTS, 128), F32)
    for i, column in enumerate(columns):
        out = jnp.where(lane == start + i, column, out)
    return out


def first_kernel(
    count_ref, f_ref, solid_ref, cell_ref, owner_ref, area_ref,
    relaxed_ref, up_ref, down_ref, table_ref, message_ref, moments,
):
    @pl.loop(0, BX)
    def _(x):
        for t in range(BY // 8):
            rows = pl.ds(t * 8, 8)
            f = [f_ref[i, x, rows, :] for i in range(NQ)]
            out, rho, jx, jy, jz = collide(f, solid_ref[x, rows, :] > 0)
            for i in range(NQ):
                relaxed_ref[i, x, rows, :] = out[i]
            at = pl.ds(pl.multiple_of(x * BY + t * 8, 8), 8)
            for q, v in enumerate((rho, jx, jy, jz)):
                moments[q, at, :] = v

    for n, (pop, dist) in enumerate(X_UP):
        x = BX - dist
        up_ref[n] = solid_ref[x].astype(F32) if pop == SOLID else relaxed_ref[pop, x]
    for n, (pop, dist) in enumerate(X_DOWN):
        x = dist - 1
        down_ref[n] = solid_ref[x].astype(F32) if pop == SOLID else relaxed_ref[pop, x]

    cell = cell_ref[...]
    owner = owner_ref[...].astype(F32)
    local_x = cell // (BY * BZ)
    local_y = (cell // BZ) % BY
    local_z = cell % BZ
    slot = lax.broadcasted_iota(jnp.int32, (1, SLOTS), 1)
    live = (slot < count_ref[0]).astype(F32)
    gx = (lax.axis_index("gx") * BX).astype(jnp.int32)
    gy = (lax.axis_index("gy") * BY).astype(jnp.int32)
    across = jnp.broadcast_to(owner, (SLOTS, SLOTS))
    same = across.T == across
    earlier = lax.broadcasted_iota(jnp.int32, (SLOTS, SLOTS), 0) < lax.broadcasted_iota(
        jnp.int32, (SLOTS, SLOTS), 1
    )
    rank = jnp.sum(jnp.where(same & earlier, 1.0, 0.0), axis=0, keepdims=True)
    place = rank * PATCH + owner
    order = (
        lax.broadcasted_iota(jnp.int32, (SLOTS, SLOTS), 0).astype(F32)
        == jnp.broadcast_to(place, (SLOTS, SLOTS))
    ).astype(F32).astype(BF16)
    exact = [
        (local_x * BY + local_y).astype(F32),
        (local_x * (BY + 8) + local_y + 4).astype(F32),
        local_z.astype(F32),
        (local_x + gx).astype(F32),
        (local_y + gy).astype(F32),
        live,
    ]
    pad = jnp.zeros((1, SLOTS), F32)
    area = area_ref[...]
    hi, mid, lo = split3(jnp.concatenate([area, jnp.zeros((5, SLOTS), F32)], axis=0))
    first = jnp.concatenate(exact + [pad, pad], axis=0).astype(BF16)
    source = jnp.concatenate(
        [v.astype(F32) for v in (first, hi, mid, lo)] + [jnp.zeros((96, SLOTS), F32)], axis=0
    ).astype(BF16)
    raw = lax.dot_general(order, source, (((1,), (1,)), ((), ())), preferred_element_type=F32)
    area_cols = [
        raw[:, 8 + k : 9 + k] + raw[:, 16 + k : 17 + k] + raw[:, 24 + k : 25 + k] for k in range(3)
    ]
    table_ref[...] = raw
    picked = sample(moments, raw, 0, BX * BY)
    fixed = [raw[:, 3:4], raw[:, 4:5], raw[:, 2:3], raw[:, 5:6]] + area_cols
    put_message(lanes_of(fixed + picked), message_ref)


def edge_kernel(relaxed_ref, solid_ref, low_ref, high_ref, up_ref, down_ref):
    low = {(pop, -dist): n for n, (pop, dist) in enumerate(X_UP)}
    high = {(pop, BX - 1 + dist): n for n, (pop, dist) in enumerate(X_DOWN)}

    def rows_of(pop, x, start, count):
        if x < 0:
            return low_ref[low[pop, x], start : start + count, :]
        if x >= BX:
            return high_ref[high[pop, x], start : start + count, :]
        if pop == SOLID:
            return solid_ref[x, start : start + count, :].astype(F32)
        return relaxed_ref[pop, x, start : start + count, :]

    for pop, x, rows, at in Y_UP:
        up_ref[at : at + rows, :] = rows_of(pop, x, BY - rows, rows)
    for pop, x, rows, at in Y_DOWN:
        down_ref[at : at + rows, :] = rows_of(pop, x, 0, rows)


def steps_kernel(
    relaxed_ref, solid_ref, low_ref, high_ref, below_ref, above_ref, table_ref,
    out_ref, up_ref, down_ref, message_ref, ext_a, ext_b, moments,
):
    for x in range(BX):
        for pop in range(NQ):
            ext_a[pop, x + HX, Y0 : Y0 + BY, :] = relaxed_ref[pop, x]
        ext_a[SOLID, x + HX, Y0 : Y0 + BY, :] = solid_ref[x].astype(F32)
    for n, (pop, dist) in enumerate(X_UP):
        ext_a[pop, HX - dist, Y0 : Y0 + BY, :] = low_ref[n]
    for n, (pop, dist) in enumerate(X_DOWN):
        ext_a[pop, HX + BX - 1 + dist, Y0 : Y0 + BY, :] = high_ref[n]
    for pop, x, rows, at in Y_UP:
        ext_a[pop, x + HX, Y0 - rows : Y0, :] = below_ref[at : at + rows, :]
    for pop, x, rows, at in Y_DOWN:
        ext_a[pop, x + HX, Y0 + BY : Y0 + BY + rows, :] = above_ref[at : at + rows, :]

    own = lax.broadcasted_iota(jnp.int32, (8, BZ), 0)

    def step(source, target, margin, which):
        @pl.loop(HX - margin, HX + BX + margin)
        def _(x):
            for t in range(5):
                row = 8 + 8 * t
                f = []
                for i in range(NQ):
                    cx, cy, cz = VEL[i]
                    v = source[i, x - cx, pl.ds(row - cy, 8), :]
                    f.append(pltpu.roll(v, cz % BZ, axis=1) if cz else v)
                solid = ext_a[SOLID, x, pl.ds(row, 8), :] > 0.0
                out, *sums = collide(f, solid)
                if target is not None:
                    for i in range(NQ):
                        target[i, x, pl.ds(row, 8), :] = out[i]
                else:
                    for i in range(NQ):
                        out_ref[i, x - HX, pl.ds(t * 8, 8), :] = out[i]

                def keep():
                    at = pl.ds(pl.multiple_of((x - HX) * (BY + 8) + t * 8, 8), 8)
                    for q, v in enumerate(sums):
                        if t == 0:
                            v = jnp.where(own >= 4, v, 0.0)
                        if t == 4:
                            v = jnp.where(own < 4, v, 0.0)
                        moments[which, q, at, :] = v

                if margin == 0:
                    keep()
                else:
                    pl.when((x >= HX) & (x < HX + BX))(keep)

    step(ext_a, ext_b, 2, 0)
    step(ext_b, ext_a, 1, 1)
    step(ext_a, None, 0, 2)
    n = 0
    m = 0
    for pop in range(NQ):
        if VEL[pop][0] > 0:
            up_ref[n] = out_ref[pop, BX - 1]
            n += 1
        if VEL[pop][0] < 0:
            down_ref[m] = out_ref[pop, 0]
            m += 1
    table = table_ref[...]
    columns = []
    for which in range(3):
        columns += sample(moments.at[which], table, 1, BX * (BY + 8))
    put_message(lanes_of(columns), message_ref)


def last_kernel(relaxed_ref, low_ref, high_ref, out_ref):
    n = 0
    m = 0
    for pop in range(NQ):
        cx, cy, cz = VEL[pop]
        for x in range(BX):
            for t in range(BY // 8):
                row = 4 + 8 * t - cy
                if x - cx < 0:
                    v = low_ref[n, row : row + 8, :]
                elif x - cx >= BX:
                    v = high_ref[m, row : row + 8, :]
                else:
                    v = relaxed_ref[pop, x - cx, row : row + 8, :]
                out_ref[pop, x, t * 8 : t * 8 + 8, :] = (
                    pltpu.roll(v, cz % BZ, axis=1) if cz else v
                )
        n += cx > 0
        m += cx < 0


def fit(fun, degree, odd):
    count = 400
    x = 0.25 + 0.25 * np.cos(np.pi * (np.arange(count) + 0.5) / count)
    powers = np.stack([x ** (2 * k + odd) for k in range(degree)], axis=1)
    weight = np.ones(count)
    best = None
    for _ in range(200):
        coef = np.linalg.lstsq(powers * weight[:, None], fun(x) * weight, rcond=None)[0]
        error = np.abs(powers @ coef - fun(x))
        if best is None or error.max() < best[0]:
            best = (error.max(), coef)
        weight = weight * (0.5 + error / error.max()) ** 0.5
        weight = weight / weight.max()
    return [float(c) for c in best[1]]


ROOT2 = math.sqrt(2.0)
SIN_POLY = fit(lambda x: ROOT2 * np.sin(np.pi * x), 5, 1)
COS_POLY = fit(lambda x: ROOT2 * np.cos(np.pi * x), 6, 0)


def horner(coefs, y):
    v = y * coefs[-1] + coefs[-2]
    for c in coefs[-3::-1]:
        v = v * y + c
    return v


def sin_cos_turns(t):
    x = t - jnp.round(t)
    y = x * x
    s = horner(SIN_POLY, y) * x
    c = horner(COS_POLY, y)
    return 1.0 - s * s, s * c


CHUNKS = NB * CAP // 128


def sum_kernel(freq_ref, first_ref, second_ref, obs_ref, out_ref, info, series, weights, acc, obs_lanes):
    lane = lax.broadcasted_iota(jnp.int32, (NB, 256), 1)
    first = first_ref[...]
    live = jnp.sum(jnp.where(lane % NV == 3, first, 0.0), axis=1, keepdims=True)
    lower = (
        lax.broadcasted_iota(jnp.int32, (NB, NB), 0) > lax.broadcasted_iota(jnp.int32, (NB, NB), 1)
    ).astype(F32).astype(BF16)
    live_lanes = jnp.broadcast_to(live, (NB, 128)).astype(BF16)
    offset = dot(lower, live_lanes)
    total = jnp.sum(live).astype(jnp.int32)
    chunks = (total + 127) // 128
    turned = [first[:, :128].T, first[:, 128:].T, second_ref[:, :128].T, second_ref[:, 128:].T]
    parts = []
    for r in range(CAP):
        at = (r % 8) * NV
        both = jnp.concatenate(
            [turned[r // 8][at : at + NV, :], turned[2 + r // 8][at : at + NV, :]], axis=0
        )
        parts.append(jnp.concatenate(split3(both), axis=0))
    lanes = lax.broadcasted_iota(jnp.int32, (NB, 128), 1).astype(F32)

    @pl.loop(0, chunks)
    def _(c):
        base = (c * 128).astype(F32)
        packed = jnp.zeros((6 * NV, 128), F32)
        for r in range(CAP):
            hot = ((offset + (float(r) - base)) == lanes) & (live_lanes.astype(F32) > float(r))
            packed = packed + dot(parts[r], jnp.where(hot, 1.0, 0.0).astype(BF16))
        value = packed[: 2 * NV] + packed[2 * NV : 4 * NV] + packed[4 * NV :]
        info[c] = value[0:8, :]
        area = [value[4 + k : 5 + k, :] for k in range(3)]
        keep = value[3:4, :]
        rows = []
        for s in range(4):
            at = 7 if s == 0 else 2 * NV // 2 + 4 * (s - 1)
            rho = value[at : at + 1, :]
            j = [value[at + 1 + k : at + 2 + k, :] for k in range(3)]
            scale = 1.0 / jnp.where(keep > 0.0, rho, 1.0)
            u = [v * scale for v in j]
            flux = u[0] * area[0] + u[1] * area[1] + u[2] * area[2]
            pressure = (rho - BASE) * (1.0 / 3.0)
            rows.append(rho * flux * keep)
            for k in range(3):
                rows.append((pressure * area[k] + j[k] * flux) * keep)
        series[c] = jnp.concatenate(rows, axis=0)

    gy = lax.axis_index("gy") * 8
    sub = lax.broadcasted_iota(jnp.int32, (8, 128), 0)
    omega = jnp.zeros((8, 128), F32)
    for k in range(8):
        omega = jnp.where(sub == k, freq_ref[gy + k], omega)
    cosines, sines = [], []
    for s in range(4):
        taper = 0.5 - 0.5 * math.cos(2.0 * math.pi * (s + 0.5) / 4)
        cosines.append(taper * jnp.cos(omega * float(s)))
        sines.append(-taper * jnp.sin(omega * float(s)))

    @pl.loop(0, chunks)
    def _(c):
        for comp in range(4):
            for part, factors in enumerate((cosines, sines)):
                v = factors[0] * series[c, comp : comp + 1, :]
                for s in range(1, 4):
                    v = v + factors[s] * series[c, 4 * s + comp : 4 * s + comp + 1, :]
                if comp == 0:
                    v = v * (1.0 / math.sqrt(3.0))
                weights[c, part * 4 + comp] = v

    observers = obs_ref[...]
    for k in range(3):
        obs_lanes[k] = jnp.broadcast_to(observers[k : k + 1, :], (128, 256)).T

    turns = [freq_ref[gy + k] * (math.sqrt(3.0) / (2.0 * math.pi)) for k in range(8)]
    over_k = [1.0 / (omega[k : k + 1, :] * math.sqrt(3.0)) for k in range(8)]
    over_k = [jnp.broadcast_to(v, (8, 128)) for v in over_k]

    @pl.loop(0, 32)
    def _(o):
        rows = pl.ds(pl.multiple_of(o * 8, 8), 8)
        place = [obs_lanes[k, rows, :] for k in range(3)]

        def body(c, carry):
            d = [place[k] - info[c, k : k + 1, :] for k in range(3)]
            square = d[0] * d[0] + d[1] * d[1] + d[2] * d[2]
            inv = lax.rsqrt(square)
            dist = square * inv
            n = [v * inv for v in d]
            out = []
            for k in range(8):
                cos, sin = sin_cos_turns(dist * turns[k])
                w = [weights[c, m, k : k + 1, :] for m in range(8)]
                re = n[0] * w[1] + n[1] * w[2] + n[2] * w[3]
                im = n[0] * w[5] + n[1] * w[6] + n[2] * w[7]
                near = inv * over_k[k]
                dr = near * re - (im + w[4])
                di = near * im + (re + w[0])
                cos = cos * inv
                sin = sin * inv
                out.append(carry[2 * k] + (cos * dr + sin * di))
                out.append(carry[2 * k + 1] + (cos * di - sin * dr))
            return tuple(out)

        sums = lax.fori_loop(0, chunks, body, tuple(jnp.zeros((8, 128), F32) for _ in range(16)))
        for k in range(8):
            acc[k, rows, :] = sums[2 * k]
            acc[8 + k, rows, :] = sums[2 * k + 1]

    ones = jnp.ones((8, 128), BF16)
    for k in range(16):
        whole = jnp.zeros((8, 256), F32)
        for piece in split3(acc[k]):
            whole = whole + lax.dot_general(
                ones, piece, (((1,), (1,)), ((), ())), preferred_element_type=F32
            )
        wave = freq_ref[gy + k % 8] * math.sqrt(3.0)
        out_ref[k // 8, k % 8 : k % 8 + 1, :] = whole[0:1, :] * wave


def call(kernel, shapes, scratch=(), smem=0, inputs=0, name=None, cost=1000):
    return pl.pallas_call(
        kernel,
        out_shape=[jax.ShapeDtypeStruct(s, F32) for s in shapes],
        in_specs=[pl.BlockSpec(memory_space=pltpu.SMEM)] * smem
        + [pl.BlockSpec(memory_space=pltpu.VMEM)] * (inputs - smem),
        out_specs=[pl.BlockSpec(memory_space=pltpu.VMEM)] * len(shapes),
        scratch_shapes=list(scratch),
        compiler_params=pltpu.CompilerParams(vmem_limit_bytes=VMEM_LIMIT),
        cost_estimate=pl.CostEstimate(flops=cost, bytes_accessed=cost, transcendentals=0),
        name=name,
    )


def ring(axis, up, down):
    count = lax.axis_size(axis)
    forward = [(i, (i + 1) % count) for i in range(count)]
    backward = [((i + 1) % count, i) for i in range(count)]
    return lax.ppermute(up, axis, forward), lax.ppermute(down, axis, backward)


def exchange(message):
    return lax.all_to_all(message, ("gx", "gy"), split_axis=0, concat_axis=0, tiled=True)


def local(
    populations, solid, panel_cell, panel_owner, panel_count, panel_area, observers, frequencies
):
    cell = panel_cell.reshape(1, SLOTS)
    owner = panel_owner.reshape(1, SLOTS)
    relaxed, up, down, table, message_a = call(
        first_kernel,
        [(NQ, BX, BY, BZ), (NXE, BY, BZ), (NXE, BY, BZ), (SLOTS, 128), (NB, 256)],
        [pltpu.VMEM((4, BX * BY, BZ), F32)],
        smem=1,
        inputs=6,
        name="first",
    )(panel_count, populations, solid, cell, owner, panel_area)
    low, high = ring("gx", up, down)
    y_up, y_down = call(edge_kernel, [(NYE, BZ)] * 2, inputs=4, name="edge")(
        relaxed, solid, low, high
    )
    below, above = ring("gy", y_up, y_down)
    got_a = exchange(message_a)
    relaxed, up, down, message_b = call(
        steps_kernel,
        [(NQ, BX, BY + 8, BZ), (5, BY + 8, BZ), (5, BY + 8, BZ), (NB, 256)],
        [
            pltpu.VMEM((NQ + 1, BX + 2 * HX, YR, BZ), F32),
            pltpu.VMEM((NQ, BX + 2 * HX, YR, BZ), F32),
            pltpu.VMEM((3, 4, BX * (BY + 8), BZ), F32),
        ],
        inputs=7,
        name="steps",
    )(relaxed, solid, low, high, below, above, table)
    got_b = exchange(message_b)
    low, high = ring("gx", up, down)
    (current,) = call(last_kernel, [(NQ, BX, BY, BZ)], inputs=3, name="last")(relaxed, low, high)
    (spectra,) = call(
        sum_kernel,
        [(2, 8, 256)],
        [
            pltpu.VMEM((CHUNKS, 8, 128), F32),
            pltpu.VMEM((CHUNKS, 16, 128), F32),
            pltpu.VMEM((CHUNKS, 8, 8, 128), F32),
            pltpu.VMEM((16, 256, 128), F32),
            pltpu.VMEM((3, 256, 128), F32),
        ],
        smem=1,
        inputs=4,
        name="sums",
    )(frequencies, got_a, got_b, observers)
    return current, spectra[None]


def solution(mesh):
    return jax.shard_map(
        local,
        mesh=mesh,
        in_specs=(
            P(None, "gx", "gy", None),
            P("gx", "gy", None),
            P(("gx", "gy")),
            P(("gx", "gy")),
            P(("gx", "gy")),
            P(None, ("gx", "gy")),
            P(),
            P(),
        ),
        out_specs=(P(None, "gx", "gy", None), P("gx", None, "gy", None)),
        check_vma=False,
    )
```

profile of v0, /device:TPU:33, one launch (start us, length us, event | category | flops | bytes accessed | tf_op | source)
XLA Modules:
  0.0 106.3 jit_solution(8058432675422565135)
XLA Ops:
  1.3 4.0 %first.1 = (f32[19,4,32,128]{3,2,1,0:T(8,128)}, f32[40,32,128]{2,1,0:T(8,128)}, f32[40,32,128]{2,1,0:T(8,128)}, f32[256,128]{1,0:T(8,128)}, f32[128,256]{1,0:T(8,128)}) custom-call(s32[1]{0:T(128)S(6)} %copy.18.count_ref, f32[19,4,32,128]{3,2,1,0:T(8,128)} %f_ref.1, s32[4,32,128]{2,1,0:T(8,128)} %solid_ref.5, s32[1,256]{1,0:T(1,128)} %bitcast.16, ...), custom_call_target="tpu_custom_call" | custom-call | flops 1000 | bytes 1000 | tf_op jit(solution)/shard_map/first/pallas_call | solution.py:540
  5.3 1.8 %collective-permute-start = (f32[40,32,128]{2,1,0:T(8,128)}, f32[40,32,128]{2,1,0:T(8,128)S(1)}, u32[]{:S(2)}, u32[]{:S(2)}) collective-permute-start(f32[40,32,128]{2,1,0:T(8,128)} %get-tuple-element.14), channel_id=1, source_target_pairs={{0,8},{8,16},{16,24},{24,32},{32,40},{40,48},{48,56},{56,64},{64,7... | collective-permute-start | bytes 1966088 | tf_op jit(solution)/shard_map/ppermute | solution.py:528
  7.0 0.0 collective-permute-start.1
  7.0 13.1 %collective-permute-done.low_ref = f32[40,32,128]{2,1,0:T(8,128)S(1)} collective-permute-done((f32[40,32,128]{2,1,0:T(8,128)}, f32[40,32,128]{2,1,0:T(8,128)S(1)}, u32[]{:S(2)}, u32[]{:S(2)}) %collective-permute-start) | collective-permute-done | bytes 655392 | tf_op jit(solution)/shard_map/ppermute | solution.py:528
  20.2 0.0 copy-start
  20.2 3.7 %collective-permute-done.1.high_ref = f32[40,32,128]{2,1,0:T(8,128)S(1)} collective-permute-done((f32[40,32,128]{2,1,0:T(8,128)}, f32[40,32,128]{2,1,0:T(8,128)S(1)}, u32[]{:S(2)}, u32[]{:S(2)}) %collective-permute-start.1) | collective-permute-done | bytes 655392 | tf_op jit(solution)/shard_map/ppermute | solution.py:528
  23.9 0.0 copy-start.1
  23.9 0.0 copy-done
  23.9 0.8 copy-done.1
  24.7 0.0 copy-start.4
  24.7 2.6 %edge.1 = (f32[480,128]{1,0:T(8,128)}, f32[480,128]{1,0:T(8,128)}) custom-call(f32[19,4,32,128]{3,2,1,0:T(8,128)} %get-tuple-element.13.relaxed_ref, s32[4,32,128]{2,1,0:T(8,128)} %solid_ref.5, f32[40,32,128]{2,1,0:T(8,128)} %copy-done, f32[40,32,128]{2,1,0:T(8,128)} %copy-done.1), custom_call_target="tpu_custom_call" | custom-call | flops 1000 | bytes 1000 | tf_op jit(solution)/shard_map/edge/pallas_call | solution.py:549
  27.3 1.3 %collective-permute-start.2 = (f32[480,128]{1,0:T(8,128)}, f32[480,128]{1,0:T(8,128)S(1)}, u32[]{:S(2)}, u32[]{:S(2)}) collective-permute-start(f32[480,128]{1,0:T(8,128)} %get-tuple-element.16), channel_id=1, source_target_pairs={{0,1},{1,2},{2,3},{3,4},{4,5},{5,6},{6,7},{7,0},{8,9},{9,10},{10,1... | collective-permute-start | bytes 737288 | tf_op jit(solution)/shard_map/ppermute | solution.py:528
  28.6 3.9 %collective-permute-start.3 = (f32[480,128]{1,0:T(8,128)}, f32[480,128]{1,0:T(8,128)S(1)}, u32[]{:S(2)}, u32[]{:S(2)}) collective-permute-start(f32[480,128]{1,0:T(8,128)} %get-tuple-element.17), channel_id=1, source_target_pairs={{1,0},{2,1},{3,2},{4,3},{5,4},{6,5},{7,6},{0,7},{9,8},{10,9},{11,1... | collective-permute-start | bytes 737288 | tf_op jit(solution)/shard_map/ppermute | solution.py:528
  32.5 0.0 copy-done.4
  32.5 0.8 copy.10
  33.3 7.8 %all-to-all-start = ((f32[128,1,256]{2,1,0:T(1,128)}), f32[128,1,256]{2,1,0:T(1,128)S(1)}, u32[]{:S(2)}, u32[]{:S(2)}) async-start(f32[128,1,256]{2,1,0:T(1,128)} %copy.10), calls=%async_computation | async-start | bytes 262144 | tf_op jit(solution)/shard_map/all_to_all | solution.py:532
  41.1 0.0 collective-permute-done.2.below_ref
  41.1 0.0 copy-start.2
  41.1 0.0 collective-permute-done.3.above_ref
  41.1 0.0 copy-start.3
  41.1 0.7 copy-done.2
  41.8 0.1 copy-done.3
  41.9 13.0 %steps.1 = (f32[19,4,40,128]{3,2,1,0:T(8,128)}, f32[5,40,128]{2,1,0:T(8,128)}, f32[5,40,128]{2,1,0:T(8,128)}, f32[128,256]{1,0:T(8,128)}) custom-call(f32[19,4,32,128]{3,2,1,0:T(8,128)} %get-tuple-element.13.relaxed_ref, s32[4,32,128]{2,1,0:T(8,128)} %solid_ref.5, f32[40,32,128]{2,1,0:T(8,128)} %copy-done, f32[40,32,128]{2,1,0:T(8,128)} %copy-done.1, ...), custom_call_target="tpu_custom_call" | custom-call | flops 1000 | bytes 1000 | tf_op jit(solution)/shard_map/steps/pallas_call | solution.py:554
  54.9 1.7 %copy.11 = f32[128,1,256]{2,1,0:T(1,128)} copy(f32[128,1,256]{2,0,1:T(8,128)} %bitcast.14) | data formatting | bytes 262144 | tf_op jit(solution)/shard_map/all_to_all | solution.py:532
  56.6 0.0 all-to-all-done
  56.6 9.8 %all-to-all-start.1 = ((f32[128,1,256]{2,1,0:T(1,128)}), f32[128,1,256]{2,1,0:T(1,128)S(1)}, u32[]{:S(2)}, u32[]{:S(2)}) async-start(f32[128,1,256]{2,1,0:T(1,128)} %copy.11), calls=%async_computation.1 | async-start | bytes 262144 | tf_op jit(solution)/shard_map/all_to_all | solution.py:532
  66.4 1.5 %collective-permute-start.4 = (f32[5,40,128]{2,1,0:T(8,128)}, f32[5,40,128]{2,1,0:T(8,128)S(1)}, u32[]{:S(2)}, u32[]{:S(2)}) collective-permute-start(f32[5,40,128]{2,1,0:T(8,128)} %get-tuple-element.20), channel_id=1, source_target_pairs={{0,8},{8,16},{16,24},{24,32},{32,40},{40,48},{48,56},{56,64},{64,7... | collective-permute-start | bytes 307208 | tf_op jit(solution)/shard_map/ppermute | solution.py:528
  67.9 0.0 collective-permute-start.5
  67.9 0.7 copy.17
  68.6 1.3 %collective-permute-done.4.low_ref = f32[5,40,128]{2,1,0:T(8,128)S(1)} collective-permute-done((f32[5,40,128]{2,1,0:T(8,128)}, f32[5,40,128]{2,1,0:T(8,128)S(1)}, u32[]{:S(2)}, u32[]{:S(2)}) %collective-permute-start.4) | collective-permute-done | bytes 102432 | tf_op jit(solution)/shard_map/ppermute | solution.py:528
  69.9 0.0 copy-start.5
  69.9 3.1 %collective-permute-done.5.high_ref = f32[5,40,128]{2,1,0:T(8,128)S(1)} collective-permute-done((f32[5,40,128]{2,1,0:T(8,128)}, f32[5,40,128]{2,1,0:T(8,128)S(1)}, u32[]{:S(2)}, u32[]{:S(2)}) %collective-permute-start.5) | collective-permute-done | bytes 102432 | tf_op jit(solution)/shard_map/ppermute | solution.py:528
  73.0 0.0 copy-start.6
  73.0 0.0 copy-done.5
  73.0 0.6 copy-done.6
  73.7 2.7 %last.1 = f32[19,4,32,128]{3,2,1,0:T(8,128)} custom-call(f32[19,4,40,128]{3,2,1,0:T(8,128)} %get-tuple-element.19.relaxed_ref, f32[5,40,128]{2,1,0:T(8,128)} %copy-done.5, f32[5,40,128]{2,1,0:T(8,128)} %copy-done.6), custom_call_target="tpu_custom_call" | custom-call | flops 1000 | bytes 1000 | tf_op jit(solution)/shard_map/last/pallas_call | solution.py:567
  76.4 0.0 all-to-all-done.1
  76.4 0.7 copy.16
  77.1 29.2 %sums.1 = f32[2,8,256]{2,1,0:T(8,128)} custom-call(f32[64]{0:T(128)} %freq_ref.1, f32[128,256]{1,0:T(8,128)} %bitcast.11, f32[128,256]{1,0:T(8,128)} %bitcast.12, f32[3,256]{1,0:T(4,128)} %obs_ref.1), custom_call_target="tpu_custom_call" | custom-call | flops 1000 | bytes 1000 | tf_op jit(solution)/shard_map/sums/pallas_call | solution.py:568
Async XLA Ops:
  5.3 14.9 %collective-permute-start = (f32[40,32,128]{2,1,0:T(8,128)}, f32[40,32,128]{2,1,0:T(8,128)S(1)}, u32[]{:S(2)}, u32[]{:S(2)}) collective-permute-start(f32[40,32,128]{2,1,0:T(8,128)} %get-tuple-element.14), channel_id=1, source_target_pairs={{0,8},{8,16},{16,24},{24,32},{32,40},{40,48},{48,56},{56,64},{64,7... | collective-permute-start | bytes 1966088 | tf_op jit(solution)/shard_map/ppermute | solution.py:528
  7.0 16.8 %collective-permute-start.1 = (f32[40,32,128]{2,1,0:T(8,128)}, f32[40,32,128]{2,1,0:T(8,128)S(1)}, u32[]{:S(2)}, u32[]{:S(2)}) collective-permute-start(f32[40,32,128]{2,1,0:T(8,128)} %get-tuple-element.15), channel_id=1, source_target_pairs={{8,0},{16,8},{24,16},{32,24},{40,32},{48,40},{56,48},{64,56},{72,6... | collective-permute-start | bytes 1966088 | tf_op jit(solution)/shard_map/ppermute | solution.py:528
  20.2 3.7 %copy-start = (f32[40,32,128]{2,1,0:T(8,128)}, f32[40,32,128]{2,1,0:T(8,128)S(1)}, u32[]{:S(2)}) copy-start(f32[40,32,128]{2,1,0:T(8,128)S(1)} %collective-permute-done.low_ref) | copy-start | bytes 1966084
  23.9 0.8 copy-start.1
  24.7 7.8 %copy-start.4 = (f32[128,256]{1,0:T(8,128)S(1)}, f32[128,256]{1,0:T(8,128)}, u32[]{:S(2)}) copy-start(f32[128,256]{1,0:T(8,128)} %get-tuple-element.22) | copy-start | bytes 393220
  27.3 13.8 %collective-permute-start.2 = (f32[480,128]{1,0:T(8,128)}, f32[480,128]{1,0:T(8,128)S(1)}, u32[]{:S(2)}, u32[]{:S(2)}) collective-permute-start(f32[480,128]{1,0:T(8,128)} %get-tuple-element.16), channel_id=1, source_target_pairs={{0,1},{1,2},{2,3},{3,4},{4,5},{5,6},{6,7},{7,0},{8,9},{9,10},{10,1... | collective-permute-start | bytes 737288 | tf_op jit(solution)/shard_map/ppermute | solution.py:528
  28.6 12.5 %collective-permute-start.3 = (f32[480,128]{1,0:T(8,128)}, f32[480,128]{1,0:T(8,128)S(1)}, u32[]{:S(2)}, u32[]{:S(2)}) collective-permute-start(f32[480,128]{1,0:T(8,128)} %get-tuple-element.17), channel_id=1, source_target_pairs={{1,0},{2,1},{3,2},{4,3},{5,4},{6,5},{7,6},{0,7},{9,8},{10,9},{11,1... | collective-permute-start | bytes 737288 | tf_op jit(solution)/shard_map/ppermute | solution.py:528
  33.3 23.3 %all-to-all-start = ((f32[128,1,256]{2,1,0:T(1,128)}), f32[128,1,256]{2,1,0:T(1,128)S(1)}, u32[]{:S(2)}, u32[]{:S(2)}) async-start(f32[128,1,256]{2,1,0:T(1,128)} %copy.10), calls=%async_computation | async-start | bytes 262144 | tf_op jit(solution)/shard_map/all_to_all | solution.py:532
  41.1 0.7 copy-start.2
  41.1 0.8 copy-start.3
  56.6 19.8 %all-to-all-start.1 = ((f32[128,1,256]{2,1,0:T(1,128)}), f32[128,1,256]{2,1,0:T(1,128)S(1)}, u32[]{:S(2)}, u32[]{:S(2)}) async-start(f32[128,1,256]{2,1,0:T(1,128)} %copy.11), calls=%async_computation.1 | async-start | bytes 262144 | tf_op jit(solution)/shard_map/all_to_all | solution.py:532
  66.4 3.5 %collective-permute-start.4 = (f32[5,40,128]{2,1,0:T(8,128)}, f32[5,40,128]{2,1,0:T(8,128)S(1)}, u32[]{:S(2)}, u32[]{:S(2)}) collective-permute-start(f32[5,40,128]{2,1,0:T(8,128)} %get-tuple-element.20), channel_id=1, source_target_pairs={{0,8},{8,16},{16,24},{24,32},{32,40},{40,48},{48,56},{56,64},{64,7... | collective-permute-start | bytes 307208 | tf_op jit(solution)/shard_map/ppermute | solution.py:528
  67.9 5.1 %collective-permute-start.5 = (f32[5,40,128]{2,1,0:T(8,128)}, f32[5,40,128]{2,1,0:T(8,128)S(1)}, u32[]{:S(2)}, u32[]{:S(2)}) collective-permute-start(f32[5,40,128]{2,1,0:T(8,128)} %get-tuple-element.21), channel_id=1, source_target_pairs={{8,0},{16,8},{24,16},{32,24},{40,32},{48,40},{56,48},{64,56},{72,6... | collective-permute-start | bytes 307208 | tf_op jit(solution)/shard_map/ppermute | solution.py:528
  69.9 3.1 %copy-start.5 = (f32[5,40,128]{2,1,0:T(8,128)}, f32[5,40,128]{2,1,0:T(8,128)S(1)}, u32[]{:S(2)}) copy-start(f32[5,40,128]{2,1,0:T(8,128)S(1)} %collective-permute-done.4.low_ref) | copy-start | bytes 307204
  73.0 0.7 copy-start.6
where the time goes:
time: 107 us; the launch traced here: 106 us
  Pallas kernels  51.6 us (48%)
  starting transfers between devices  26.1 us (24%)
  waiting for transfers between devices  21.2 us (20%)
  local copies, waits for them, and re-layouts  6.03 us (6%)
  between operations  1.34 us (1%)
    pallas_call x1, Pallas kernels, local(): call(sum_kernel, [(2, 8, 256)], [pltpu.VMEM((CHUNKS, 8, 128), F32), pltpu...  29.2 us
    ppermute x6, waiting for transfers between devices, ring(): return (lax.ppermute(up, axis, forward), lax.ppermute(down, axis, backward))  21.2 us
    all_to_all x2, starting transfers between devices, exchange(): lax.all_to_all(message, ('gx', 'gy'), split_axis=0, concat_axis=0, tiled=...  17.6 us
    pallas_call x1, Pallas kernels, local(): call(steps_kernel, [(NQ, BX, BY + 8, BZ), (5, BY + 8, BZ), (5, BY + 8, BZ...  13 us
    ppermute x6, starting transfers between devices, ring(): return (lax.ppermute(up, axis, forward), lax.ppermute(down, axis, backward))  8.51 us
    pallas_call x1, Pallas kernels, local(): call(first_kernel, [(NQ, BX, BY, BZ), (NXE, BY, BZ), (NXE, BY, BZ), (SLOT...  4 us
    unnamed x16, local copies, waits for them, and re-layouts  3.56 us
    pallas_call x1, Pallas kernels, local(): call(last_kernel, [(NQ, BX, BY, BZ)], inputs=3, name='last')  2.73 us
  transfers between devices with their start and end apart: 8, of which 4 were waited for; matrix products, arithmetic and copies ran while one was open for 3% of the time, Pallas kernels for 15%

commit v1 on v0

--- a/solution.py
+++ b/solution.py
@@ -1,4 +1,3 @@
-import functools
 import math
 
 import jax
@@ -8,6 +7,7 @@
 from jax.experimental import pallas as pl
 from jax.experimental.pallas import tpu as pltpu
 from jax.sharding import PartitionSpec as P
+
 
 F32 = jnp.float32
 BF16 = jnp.bfloat16
@@ -29,7 +29,6 @@
 NB = 128
 NV = 16
 BASE = 19.0
-VMEM_LIMIT = 60 * 1024 * 1024
 
 
 def x_entries(side):
@@ -151,16 +150,21 @@
 
 
 def put_message(values, out_ref):
+    halves = []
     for part in range(2):
         total = jnp.zeros((PATCH, 128), F32)
         for r in range(8):
             at = (part * 8 + r) * PATCH
             block = values[at : at + PATCH, :]
             total = total + (pltpu.roll(block, r * NV, axis=1) if r else block)
-        for p in range(PATCH):
-            out_ref[p * 8 : p * 8 + 8, part * 128 : part * 128 + 128] = jnp.broadcast_to(
-                total[p : p + 1, :], (8, 128)
-            )
+        halves.append(total)
+    odd = lax.broadcasted_iota(jnp.int32, (16, 128), 0) % 2 == 1
+    for p in range(PATCH):
+        out_ref[p * 16 : p * 16 + 16, :] = jnp.where(
+            odd,
+            jnp.broadcast_to(halves[1][p : p + 1, :], (16, 128)),
+            jnp.broadcast_to(halves[0][p : p + 1, :], (16, 128)),
+        )
 
 
 def lanes_of(columns, start=0):
@@ -171,21 +175,23 @@
     return out
 
 
-def first_kernel(
-    count_ref, f_ref, solid_ref, cell_ref, owner_ref, area_ref,
-    relaxed_ref, up_ref, down_ref, table_ref, message_ref, moments,
-):
+def turn(v, pop):
+    step = VEL[pop][2]
+    return pltpu.roll(v, step % BZ, axis=1) if step else v
+
+
+def first_kernel(f_ref, solid_ref, relaxed_ref, up_ref, down_ref, moments_ref):
     @pl.loop(0, BX)
     def _(x):
         for t in range(BY // 8):
             rows = pl.ds(t * 8, 8)
             f = [f_ref[i, x, rows, :] for i in range(NQ)]
-            out, rho, jx, jy, jz = collide(f, solid_ref[x, rows, :] > 0)
+            out, *sums = collide(f, solid_ref[x, rows, :] > 0)
             for i in range(NQ):
-                relaxed_ref[i, x, rows, :] = out[i]
+                relaxed_ref[i, x, rows, :] = turn(out[i], i)
             at = pl.ds(pl.multiple_of(x * BY + t * 8, 8), 8)
-            for q, v in enumerate((rho, jx, jy, jz)):
-                moments[q, at, :] = v
+            for q, v in enumerate(sums):
+                moments_ref[q, at, :] = v
 
     for n, (pop, dist) in enumerate(X_UP):
         x = BX - dist
@@ -194,6 +200,8 @@
         x = dist - 1
         down_ref[n] = solid_ref[x].astype(F32) if pop == SOLID else relaxed_ref[pop, x]
 
+
+def slots_kernel(count_ref, cell_ref, owner_ref, area_ref, moments_ref, table_ref, message_ref):
     cell = cell_ref[...]
     owner = owner_ref[...].astype(F32)
     local_x = cell // (BY * BZ)
@@ -234,7 +242,7 @@
         raw[:, 8 + k : 9 + k] + raw[:, 16 + k : 17 + k] + raw[:, 24 + k : 25 + k] for k in range(3)
     ]
     table_ref[...] = raw
-    picked = sample(moments, raw, 0, BX * BY)
+    picked = sample([moments_ref[q] for q in range(4)], raw, 0, BX * BY)
     fixed = [raw[:, 3:4], raw[:, 4:5], raw[:, 2:3], raw[:, 5:6]] + area_cols
     put_message(lanes_of(fixed + picked), message_ref)
 
@@ -284,31 +292,24 @@
                 row = 8 + 8 * t
                 f = []
                 for i in range(NQ):
-                    cx, cy, cz = VEL[i]
-                    v = source[i, x - cx, pl.ds(row - cy, 8), :]
-                    f.append(pltpu.roll(v, cz % BZ, axis=1) if cz else v)
+                    cx, cy, _ = VEL[i]
+                    f.append(source[i, x - cx, pl.ds(row - cy, 8), :])
                 solid = ext_a[SOLID, x, pl.ds(row, 8), :] > 0.0
                 out, *sums = collide(f, solid)
                 if target is not None:
                     for i in range(NQ):
-                        target[i, x, pl.ds(row, 8), :] = out[i]
+                        target[i, x, pl.ds(row, 8), :] = turn(out[i], i)
                 else:
                     for i in range(NQ):
-                        out_ref[i, x - HX, pl.ds(t * 8, 8), :] = out[i]
-
-                def keep():
-                    at = pl.ds(pl.multiple_of((x - HX) * (BY + 8) + t * 8, 8), 8)
-                    for q, v in enumerate(sums):
-                        if t == 0:
-                            v = jnp.where(own >= 4, v, 0.0)
-                        if t == 4:
-                            v = jnp.where(own < 4, v, 0.0)
-                        moments[which, q, at, :] = v
-
-                if margin == 0:
-                    keep()
-                else:
-                    pl.when((x >= HX) & (x < HX + BX))(keep)
+                        out_ref[i, x - HX, pl.ds(t * 8, 8), :] = turn(out[i], i)
+
+                at = pl.ds(pl.multiple_of(x * (BY + 8) + t * 8, 8), 8)
+                for q, v in enumerate(sums):
+                    if t == 0:
+                        v = jnp.where(own >= 4, v, 0.0)
+                    if t == 4:
+                        v = jnp.where(own < 4, v, 0.0)
+                    moments[which, q, at, :] = v
 
     step(ext_a, ext_b, 2, 0)
     step(ext_b, ext_a, 1, 1)
@@ -325,7 +326,9 @@
     table = table_ref[...]
     columns = []
     for which in range(3):
-        columns += sample(moments.at[which], table, 1, BX * (BY + 8))
+        inside = pl.ds(HX * (BY + 8), BX * (BY + 8))
+        sums = [moments[which, q, inside, :] for q in range(4)]
+        columns += sample(sums, table, 1, BX * (BY + 8))
     put_message(lanes_of(columns), message_ref)
 
 
@@ -333,7 +336,7 @@
     n = 0
     m = 0
     for pop in range(NQ):
-        cx, cy, cz = VEL[pop]
+        cx, cy, _ = VEL[pop]
         for x in range(BX):
             for t in range(BY // 8):
                 row = 4 + 8 * t - cy
@@ -343,9 +346,7 @@
                     v = high_ref[m, row : row + 8, :]
                 else:
                     v = relaxed_ref[pop, x - cx, row : row + 8, :]
-                out_ref[pop, x, t * 8 : t * 8 + 8, :] = (
-                    pltpu.roll(v, cz % BZ, axis=1) if cz else v
-                )
+                out_ref[pop, x, t * 8 : t * 8 + 8, :] = v
         n += cx > 0
         m += cx < 0
 
@@ -368,7 +369,7 @@
 
 ROOT2 = math.sqrt(2.0)
 SIN_POLY = fit(lambda x: ROOT2 * np.sin(np.pi * x), 5, 1)
-COS_POLY = fit(lambda x: ROOT2 * np.cos(np.pi * x), 6, 0)
+COS_POLY = fit(lambda x: ROOT2 * np.cos(np.pi * x), 5, 0)
 
 
 def horner(coefs, y):
@@ -389,34 +390,36 @@
 CHUNKS = NB * CAP // 128
 
 
-def sum_kernel(freq_ref, first_ref, second_ref, obs_ref, out_ref, info, series, weights, acc, obs_lanes):
-    lane = lax.broadcasted_iota(jnp.int32, (NB, 256), 1)
+def sum_kernel(
+    freq_ref, first_ref, second_ref, obs_ref, out_ref, info, series, weights, acc, obs_lanes, places
+):
+    lane = lax.broadcasted_iota(jnp.int32, (2 * NB, 128), 1)
     first = first_ref[...]
     live = jnp.sum(jnp.where(lane % NV == 3, first, 0.0), axis=1, keepdims=True)
     lower = (
-        lax.broadcasted_iota(jnp.int32, (NB, NB), 0) > lax.broadcasted_iota(jnp.int32, (NB, NB), 1)
+        lax.broadcasted_iota(jnp.int32, (2 * NB, 2 * NB), 0)
+        > lax.broadcasted_iota(jnp.int32, (2 * NB, 2 * NB), 1)
     ).astype(F32).astype(BF16)
-    live_lanes = jnp.broadcast_to(live, (NB, 128)).astype(BF16)
-    offset = dot(lower, live_lanes)
+    live_lanes = jnp.broadcast_to(live, (2 * NB, 128))
+    offset = dot(lower, live_lanes.astype(BF16))
     total = jnp.sum(live).astype(jnp.int32)
     chunks = (total + 127) // 128
-    turned = [first[:, :128].T, first[:, 128:].T, second_ref[:, :128].T, second_ref[:, 128:].T]
+    for r in range(8):
+        places[r] = jnp.where(live_lanes > float(r), offset + float(r), -1.0)
+    turned = [first.T, second_ref[...].T]
     parts = []
-    for r in range(CAP):
-        at = (r % 8) * NV
-        both = jnp.concatenate(
-            [turned[r // 8][at : at + NV, :], turned[2 + r // 8][at : at + NV, :]], axis=0
-        )
+    for r in range(8):
+        both = jnp.concatenate([v[r * NV : r * NV + NV, :] for v in turned], axis=0)
         parts.append(jnp.concatenate(split3(both), axis=0))
-    lanes = lax.broadcasted_iota(jnp.int32, (NB, 128), 1).astype(F32)
+    lanes = lax.broadcasted_iota(jnp.int32, (2 * NB, 128), 1)
 
     @pl.loop(0, chunks)
     def _(c):
-        base = (c * 128).astype(F32)
+        here = (lanes + c * 128).astype(F32)
         packed = jnp.zeros((6 * NV, 128), F32)
-        for r in range(CAP):
-            hot = ((offset + (float(r) - base)) == lanes) & (live_lanes.astype(F32) > float(r))
-            packed = packed + dot(parts[r], jnp.where(hot, 1.0, 0.0).astype(BF16))
+        for r in range(8):
+            hot = jnp.where(places[r] == here, 1.0, 0.0).astype(BF16)
+            packed = packed + dot(parts[r], hot)
         value = packed[: 2 * NV] + packed[2 * NV : 4 * NV] + packed[4 * NV :]
         info[c] = value[0:8, :]
         area = [value[4 + k : 5 + k, :] for k in range(3)]
@@ -507,7 +510,7 @@
         out_ref[k // 8, k % 8 : k % 8 + 1, :] = whole[0:1, :] * wave
 
 
-def call(kernel, shapes, scratch=(), smem=0, inputs=0, name=None, cost=1000):
+def call(kernel, shapes, scratch=(), smem=0, inputs=0, cost=1000, limit=8):
     return pl.pallas_call(
         kernel,
         out_shape=[jax.ShapeDtypeStruct(s, F32) for s in shapes],
@@ -515,9 +518,8 @@
         + [pl.BlockSpec(memory_space=pltpu.VMEM)] * (inputs - smem),
         out_specs=[pl.BlockSpec(memory_space=pltpu.VMEM)] * len(shapes),
         scratch_shapes=list(scratch),
-        compiler_params=pltpu.CompilerParams(vmem_limit_bytes=VMEM_LIMIT),
+        compiler_params=pltpu.CompilerParams(vmem_limit_bytes=limit << 20),
         cost_estimate=pl.CostEstimate(flops=cost, bytes_accessed=cost, transcendentals=0),
-        name=name,
     )
 
 
@@ -525,46 +527,47 @@
     count = lax.axis_size(axis)
     forward = [(i, (i + 1) % count) for i in range(count)]
     backward = [((i + 1) % count, i) for i in range(count)]
-    return lax.ppermute(up, axis, forward), lax.ppermute(down, axis, backward)
+    low = lax.ppermute(up, axis, forward)
+    high = lax.ppermute(down, axis, backward)
+    return low, high
 
 
 def exchange(message):
     return lax.all_to_all(message, ("gx", "gy"), split_axis=0, concat_axis=0, tiled=True)
 
 
-def local(
+def run(
     populations, solid, panel_cell, panel_owner, panel_count, panel_area, observers, frequencies
 ):
     cell = panel_cell.reshape(1, SLOTS)
     owner = panel_owner.reshape(1, SLOTS)
-    relaxed, up, down, table, message_a = call(
+    relaxed, up, down, moments = call(
         first_kernel,
-        [(NQ, BX, BY, BZ), (NXE, BY, BZ), (NXE, BY, BZ), (SLOTS, 128), (NB, 256)],
-        [pltpu.VMEM((4, BX * BY, BZ), F32)],
-        smem=1,
-        inputs=6,
-        name="first",
-    )(panel_count, populations, solid, cell, owner, panel_area)
+        [(NQ, BX, BY, BZ), (NXE, BY, BZ), (NXE, BY, BZ), (4, BX * BY, BZ)],
+        inputs=2,
+        limit=12,
+    )(populations, solid)
+    table, message_a = call(
+        slots_kernel, [(SLOTS, 128), (2 * NB, 128)], smem=1, inputs=5
+    )(panel_count, cell, owner, panel_area, moments)
     low, high = ring("gx", up, down)
-    y_up, y_down = call(edge_kernel, [(NYE, BZ)] * 2, inputs=4, name="edge")(
-        relaxed, solid, low, high
-    )
+    y_up, y_down = call(edge_kernel, [(NYE, BZ)] * 2, inputs=4)(relaxed, solid, low, high)
     below, above = ring("gy", y_up, y_down)
     got_a = exchange(message_a)
     relaxed, up, down, message_b = call(
         steps_kernel,
-        [(NQ, BX, BY + 8, BZ), (5, BY + 8, BZ), (5, BY + 8, BZ), (NB, 256)],
+        [(NQ, BX, BY + 8, BZ), (5, BY + 8, BZ), (5, BY + 8, BZ), (2 * NB, 128)],
         [
             pltpu.VMEM((NQ + 1, BX + 2 * HX, YR, BZ), F32),
             pltpu.VMEM((NQ, BX + 2 * HX, YR, BZ), F32),
-            pltpu.VMEM((3, 4, BX * (BY + 8), BZ), F32),
+            pltpu.VMEM((3, 4, (BX + 2 * HX) * (BY + 8), BZ), F32),
         ],
         inputs=7,
-        name="steps",
+        limit=28,
     )(relaxed, solid, low, high, below, above, table)
     got_b = exchange(message_b)
     low, high = ring("gx", up, down)
-    (current,) = call(last_kernel, [(NQ, BX, BY, BZ)], inputs=3, name="last")(relaxed, low, high)
+    (current,) = call(last_kernel, [(NQ, BX, BY, BZ)], inputs=3)(relaxed, low, high)
     (spectra,) = call(
         sum_kernel,
         [(2, 8, 256)],
@@ -574,17 +577,18 @@
             pltpu.VMEM((CHUNKS, 8, 8, 128), F32),
             pltpu.VMEM((16, 256, 128), F32),
             pltpu.VMEM((3, 256, 128), F32),
+            pltpu.VMEM((8, 2 * NB, 128), F32),
         ],
         smem=1,
         inputs=4,
-        name="sums",
+        limit=14,
     )(frequencies, got_a, got_b, observers)
     return current, spectra[None]
 
 
 def solution(mesh):
     return jax.shard_map(
-        local,
+        run,
         mesh=mesh,
         in_specs=(
             P(None, "gx", "gy", None),

time: 107 us -> 95.2 us (0.89)
  the two profiles are of different devices: /device:TPU:33 before, /device:TPU:0 now
where the time goes in v1:
time: 95.2 us; the launch traced here: 94.9 us
  Pallas kernels  39.6 us (42%)
  starting transfers between devices  31.9 us (34%)
  waiting for transfers between devices  16.7 us (18%)
  local copies, waits for them, and re-layouts  5.35 us (6%)
  between operations  1.41 us (1%)
    pallas_call x1, Pallas kernels, run(): call(sum_kernel, [(2, 8, 256)], [pltpu.VMEM((CHUNKS, 8, 128), F32), pltpu...  28.4 us
    all_to_all x2, starting transfers between devices, exchange(): lax.all_to_all(message, ('gx', 'gy'), split_axis=0, concat_axis=0, tiled=...  17.7 us
    ppermute x3, waiting for transfers between devices, ring(): low = lax.ppermute(up, axis, forward)  15.6 us
    ppermute x3, starting transfers between devices, ring(): high = lax.ppermute(down, axis, backward)  12.5 us
    pallas_call x1, Pallas kernels, run(): call(steps_kernel, [(NQ, BX, BY + 8, BZ), (5, BY + 8, BZ), (5, BY + 8, BZ...  6.57 us
    unnamed x22, local copies, waits for them, and re-layouts  5.35 us
  transfers between devices with their start and end apart: 8, of which 3 were waited for; matrix products, arithmetic and copies ran while one was open for 0% of the time, Pallas kernels for 10%

profile of v1, /device:TPU:0, one launch (start us, length us, event | category | flops | bytes accessed | tf_op | source)
XLA Modules:
  0.0 94.9 jit_solution(7161235432929414868)
XLA Ops:
  0.6 0.0 copy-start.2
  0.6 1.3 %copy-done.2 = f32[19,4,32,128]{3,2,1,0:T(8,128)S(1)} copy-done((f32[19,4,32,128]{3,2,1,0:T(8,128)S(1)}, f32[19,4,32,128]{3,2,1,0:T(8,128)}, u32[]{:S(2)}) %copy-start.2) | copy-done | bytes 1245208
  1.9 0.0 copy-start.3
  1.9 0.8 copy-done.3
  2.8 0.9 shard_map.95
  3.6 0.1 collective-permute-start
  3.7 4.6 %collective-permute-start.1 = (f32[40,32,128]{2,1,0:T(8,128)S(1)}, f32[40,32,128]{2,1,0:T(8,128)S(1)}, u32[]{:S(2)}, u32[]{:S(2)}) collective-permute-start(f32[40,32,128]{2,1,0:T(8,128)S(1)} %get-tuple-element.16), channel_id=1, source_target_pairs={{8,0},{16,8},{24,16},{32,24},{40,32},{48,40},{56,48},{64,56},{72,6... | collective-permute-start | bytes 1966088 | tf_op jit(solution)/shard_map/ppermute | solution.py:531
  8.3 12.6 %collective-permute-done.low_ref = f32[40,32,128]{2,1,0:T(8,128)S(1)} collective-permute-done((f32[40,32,128]{2,1,0:T(8,128)S(1)}, f32[40,32,128]{2,1,0:T(8,128)S(1)}, u32[]{:S(2)}, u32[]{:S(2)}) %collective-permute-start) | collective-permute-done | bytes 655392 | tf_op jit(solution)/shard_map/ppermute | solution.py:530
  20.9 0.0 collective-permute-done.1.high_ref
  20.9 0.0 copy-start.5
  20.9 0.0 copy-start.7
  20.9 0.0 copy-start.8
  20.9 0.0 copy-start.4
  20.9 0.9 shard_map.96
  21.9 1.6 %collective-permute-start.2 = (f32[480,128]{1,0:T(8,128)}, f32[480,128]{1,0:T(8,128)S(1)}, u32[]{:S(2)}, u32[]{:S(2)}) collective-permute-start(f32[480,128]{1,0:T(8,128)} %get-tuple-element.17), channel_id=1, source_target_pairs={{0,1},{1,2},{2,3},{3,4},{4,5},{5,6},{6,7},{7,0},{8,9},{9,10},{10,1... | collective-permute-start | bytes 737288 | tf_op jit(solution)/shard_map/ppermute | solution.py:530
  23.4 4.1 %collective-permute-start.3 = (f32[480,128]{1,0:T(8,128)}, f32[480,128]{1,0:T(8,128)S(1)}, u32[]{:S(2)}, u32[]{:S(2)}) collective-permute-start(f32[480,128]{1,0:T(8,128)} %get-tuple-element.18), channel_id=1, source_target_pairs={{1,0},{2,1},{3,2},{4,3},{5,4},{6,5},{7,6},{0,7},{9,8},{10,9},{11,1... | collective-permute-start | bytes 737288 | tf_op jit(solution)/shard_map/ppermute | solution.py:531
  28.2 0.0 copy-done.5
  28.2 0.0 copy-done.7
  28.2 0.0 copy-done.8
  28.2 1.7 %shard_map.97 = (f32[256,128]{1,0:T(8,128)S(1)}, f32[256,128]{1,0:T(8,128)}) custom-call(s32[1]{0:T(128)S(6)} %copy.10.count_ref, s32[1,256]{1,0:T(1,128)S(1)} %bitcast.9, s32[1,256]{1,0:T(1,128)S(1)} %bitcast.10, f32[3,256]{1,0:T(4,128)S(1)} %copy-done.5, f32[4,128,128]{2,1,0:T(8,128)S(1)} %get-tuple-element.19.moments_ref), custom_call_target="tpu_custom_call" | custom-call | flops 1000 | bytes 1000 | tf_op jit(solution)/shard_map/pallas_call | solution.py:550
  29.9 9.0 %all-to-all-start = ((f32[128,2,128]{2,1,0:T(2,128)}), f32[128,2,128]{2,1,0:T(2,128)S(1)}, u32[]{:S(2)}, u32[]{:S(2)}) async-start(f32[128,2,128]{2,1,0:T(2,128)} %bitcast.2), calls=%async_computation | async-start | bytes 262144 | tf_op jit(solution)/shard_map/all_to_all | solution.py:536
  38.9 0.0 collective-permute-done.2.below_ref
  38.9 0.0 collective-permute-done.3.above_ref
  38.9 0.0 copy-done.4
  38.9 6.6 %shard_map.98 = (f32[19,4,40,128]{3,2,1,0:T(8,128)S(1)}, f32[5,40,128]{2,1,0:T(8,128)S(1)}, f32[5,40,128]{2,1,0:T(8,128)S(1)}, f32[256,128]{1,0:T(8,128)}) custom-call(f32[19,4,32,128]{3,2,1,0:T(8,128)S(1)} %get-tuple-element.14.relaxed_ref, s32[4,32,128]{2,1,0:T(8,128)S(1)} %copy-done.4, f32[40,32,128]{2,1,0:T(8,128)S(1)} %collective-permute-done.low_ref, ...), custom_call_target="tpu_custom_call" | custom-call | flops 1000 | bytes 1000 | tf_op jit(solution)/shard_map/pallas_call | solution.py:557
  45.5 0.0 copy-start
  45.5 1.2 %copy-done = f32[19,4,40,128]{3,2,1,0:T(8,128)} copy-done((f32[19,4,40,128]{3,2,1,0:T(8,128)}, f32[19,4,40,128]{3,2,1,0:T(8,128)S(1)}, u32[]{:S(2)}) %copy-start) | copy-done | bytes 1556504
  46.6 0.0 copy-start.10
  46.6 0.6 copy-done.10
  47.3 1.1 %all-to-all-done = f32[128,2,128]{2,1,0:T(2,128)S(1)} async-done(((f32[128,2,128]{2,1,0:T(2,128)}), f32[128,2,128]{2,1,0:T(2,128)S(1)}, u32[]{:S(2)}, u32[]{:S(2)}) %all-to-all-start) | async-done | bytes 131104 | tf_op jit(solution)/shard_map/all_to_all | solution.py:536
  48.3 8.7 %all-to-all-start.1 = ((f32[128,2,128]{2,1,0:T(2,128)}), f32[128,2,128]{2,1,0:T(2,128)S(1)}, u32[]{:S(2)}, u32[]{:S(2)}) async-start(f32[128,2,128]{2,1,0:T(2,128)} %bitcast.4), calls=%async_computation.1 | async-start | bytes 262144 | tf_op jit(solution)/shard_map/all_to_all | solution.py:536
  57.0 0.1 collective-permute-start.4
  57.1 3.8 %collective-permute-start.5 = (f32[5,40,128]{2,1,0:T(8,128)S(1)}, f32[5,40,128]{2,1,0:T(8,128)S(1)}, u32[]{:S(2)}, u32[]{:S(2)}) collective-permute-start(f32[5,40,128]{2,1,0:T(8,128)S(1)} %get-tuple-element.23), channel_id=1, source_target_pairs={{8,0},{16,8},{24,16},{32,24},{40,32},{48,40},{56,48},{64,56},{72,6... | collective-permute-start | bytes 307208 | tf_op jit(solution)/shard_map/ppermute | solution.py:531
  61.0 3.0 %collective-permute-done.4.low_ref = f32[5,40,128]{2,1,0:T(8,128)S(1)} collective-permute-done((f32[5,40,128]{2,1,0:T(8,128)}, f32[5,40,128]{2,1,0:T(8,128)S(1)}, u32[]{:S(2)}, u32[]{:S(2)}) %collective-permute-start.4) | collective-permute-done | bytes 102432 | tf_op jit(solution)/shard_map/ppermute | solution.py:530
  64.0 0.0 collective-permute-done.5.high_ref
  64.0 0.0 copy-start.1
  64.0 1.4 %copy-done.1 = f32[19,4,40,128]{3,2,1,0:T(8,128)S(1)} copy-done((f32[19,4,40,128]{3,2,1,0:T(8,128)S(1)}, f32[19,4,40,128]{3,2,1,0:T(8,128)}, u32[]{:S(2)}) %copy-start.1) | copy-done | bytes 1556504
  65.4 0.0 copy-start.6
  65.4 0.0 copy-start.9
  65.4 1.1 %shard_map.99 = f32[19,4,32,128]{3,2,1,0:T(8,128)} custom-call(f32[19,4,40,128]{3,2,1,0:T(8,128)S(1)} %copy-done.1, f32[5,40,128]{2,1,0:T(8,128)S(1)} %collective-permute-done.4.low_ref, f32[5,40,128]{2,1,0:T(8,128)S(1)} %collective-permute-done.5.high_ref), custom_call_target="tpu_custom_call" | custom-call | flops 1000 | bytes 1000 | tf_op jit(solution)/shard_map/pallas_call | solution.py:570
  66.5 0.0 all-to-all-done.1
  66.5 0.0 copy-done.6
  66.5 0.0 copy-done.9
  66.5 28.4 %shard_map.100 = f32[2,8,256]{2,1,0:T(8,128)} custom-call(f32[64]{0:T(128)S(1)} %copy-done.9, f32[256,128]{1,0:T(8,128)S(1)} %bitcast.7, f32[256,128]{1,0:T(8,128)S(1)} %bitcast.8, f32[3,256]{1,0:T(4,128)S(1)} %copy-done.6), custom_call_target="tpu_custom_call" | custom-call | flops 1000 | bytes 1000 | tf_op jit(solution)/shard_map/pallas_call | solution.py:571
Async XLA Ops:
  0.6 1.3 %copy-start.2 = (f32[19,4,32,128]{3,2,1,0:T(8,128)S(1)}, f32[19,4,32,128]{3,2,1,0:T(8,128)}, u32[]{:S(2)}) copy-start(f32[19,4,32,128]{3,2,1,0:T(8,128)} %f_ref.1) | copy-start | bytes 3735556
  1.9 0.8 copy-start.3
  3.6 17.3 %collective-permute-start = (f32[40,32,128]{2,1,0:T(8,128)S(1)}, f32[40,32,128]{2,1,0:T(8,128)S(1)}, u32[]{:S(2)}, u32[]{:S(2)}) collective-permute-start(f32[40,32,128]{2,1,0:T(8,128)S(1)} %get-tuple-element.15), channel_id=1, source_target_pairs={{0,8},{8,16},{16,24},{24,32},{32,40},{40,48},{48,56},{56,64},{64,7... | collective-permute-start | bytes 1966088 | tf_op jit(solution)/shard_map/ppermute | solution.py:530
  3.7 17.2 %collective-permute-start.1 = (f32[40,32,128]{2,1,0:T(8,128)S(1)}, f32[40,32,128]{2,1,0:T(8,128)S(1)}, u32[]{:S(2)}, u32[]{:S(2)}) collective-permute-start(f32[40,32,128]{2,1,0:T(8,128)S(1)} %get-tuple-element.16), channel_id=1, source_target_pairs={{8,0},{16,8},{24,16},{32,24},{40,32},{48,40},{56,48},{64,56},{72,6... | collective-permute-start | bytes 1966088 | tf_op jit(solution)/shard_map/ppermute | solution.py:531
  20.9 7.2 %copy-start.5 = (f32[3,256]{1,0:T(4,128)S(1)}, f32[3,256]{1,0:T(4,128)}, u32[]{:S(2)}) copy-start(f32[3,256]{1,0:T(4,128)} %area_ref.1) | copy-start | bytes 9220
  20.9 7.3 %copy-start.7 = (s32[256]{0:T(256)S(1)}, s32[256]{0:T(256)}, u32[]{:S(2)}) copy-start(s32[256]{0:T(256)} %param.10) | copy-start | bytes 3076
  20.9 7.3 %copy-start.8 = (s32[256]{0:T(256)S(1)}, s32[256]{0:T(256)}, u32[]{:S(2)}) copy-start(s32[256]{0:T(256)} %param.11) | copy-start | bytes 3076
  20.9 18.0 %copy-start.4 = (s32[4,32,128]{2,1,0:T(8,128)S(1)}, s32[4,32,128]{2,1,0:T(8,128)}, u32[]{:S(2)}) copy-start(s32[4,32,128]{2,1,0:T(8,128)} %solid_ref.5) | copy-start | bytes 196612
  21.9 17.0 %collective-permute-start.2 = (f32[480,128]{1,0:T(8,128)}, f32[480,128]{1,0:T(8,128)S(1)}, u32[]{:S(2)}, u32[]{:S(2)}) collective-permute-start(f32[480,128]{1,0:T(8,128)} %get-tuple-element.17), channel_id=1, source_target_pairs={{0,1},{1,2},{2,3},{3,4},{4,5},{5,6},{6,7},{7,0},{8,9},{9,10},{10,1... | collective-permute-start | bytes 737288 | tf_op jit(solution)/shard_map/ppermute | solution.py:530
  23.4 15.4 %collective-permute-start.3 = (f32[480,128]{1,0:T(8,128)}, f32[480,128]{1,0:T(8,128)S(1)}, u32[]{:S(2)}, u32[]{:S(2)}) collective-permute-start(f32[480,128]{1,0:T(8,128)} %get-tuple-element.18), channel_id=1, source_target_pairs={{1,0},{2,1},{3,2},{4,3},{5,4},{6,5},{7,6},{0,7},{9,8},{10,9},{11,1... | collective-permute-start | bytes 737288 | tf_op jit(solution)/shard_map/ppermute | solution.py:531
  29.9 18.4 %all-to-all-start = ((f32[128,2,128]{2,1,0:T(2,128)}), f32[128,2,128]{2,1,0:T(2,128)S(1)}, u32[]{:S(2)}, u32[]{:S(2)}) async-start(f32[128,2,128]{2,1,0:T(2,128)} %bitcast.2), calls=%async_computation | async-start | bytes 262144 | tf_op jit(solution)/shard_map/all_to_all | solution.py:536
  45.5 1.2 %copy-start = (f32[19,4,40,128]{3,2,1,0:T(8,128)}, f32[19,4,40,128]{3,2,1,0:T(8,128)S(1)}, u32[]{:S(2)}) copy-start(f32[19,4,40,128]{3,2,1,0:T(8,128)S(1)} %get-tuple-element.21.relaxed_ref) | copy-start | bytes 4669444
  46.6 0.6 copy-start.10
  48.3 18.2 %all-to-all-start.1 = ((f32[128,2,128]{2,1,0:T(2,128)}), f32[128,2,128]{2,1,0:T(2,128)S(1)}, u32[]{:S(2)}, u32[]{:S(2)}) async-start(f32[128,2,128]{2,1,0:T(2,128)} %bitcast.4), calls=%async_computation.1 | async-start | bytes 262144 | tf_op jit(solution)/shard_map/all_to_all | solution.py:536
  57.0 6.9 %collective-permute-start.4 = (f32[5,40,128]{2,1,0:T(8,128)}, f32[5,40,128]{2,1,0:T(8,128)S(1)}, u32[]{:S(2)}, u32[]{:S(2)}) collective-permute-start(f32[5,40,128]{2,1,0:T(8,128)} %copy-done.10), channel_id=1, source_target_pairs={{0,8},{8,16},{16,24},{24,32},{32,40},{40,48},{48,56},{56,64},{64,7... | collective-permute-start | bytes 307208 | tf_op jit(solution)/shard_map/ppermute | solution.py:530
  57.1 6.9 %collective-permute-start.5 = (f32[5,40,128]{2,1,0:T(8,128)S(1)}, f32[5,40,128]{2,1,0:T(8,128)S(1)}, u32[]{:S(2)}, u32[]{:S(2)}) collective-permute-start(f32[5,40,128]{2,1,0:T(8,128)S(1)} %get-tuple-element.23), channel_id=1, source_target_pairs={{8,0},{16,8},{24,16},{32,24},{40,32},{48,40},{56,48},{64,56},{72,6... | collective-permute-start | bytes 307208 | tf_op jit(solution)/shard_map/ppermute | solution.py:531
  64.0 1.4 %copy-start.1 = (f32[19,4,40,128]{3,2,1,0:T(8,128)S(1)}, f32[19,4,40,128]{3,2,1,0:T(8,128)}, u32[]{:S(2)}) copy-start(f32[19,4,40,128]{3,2,1,0:T(8,128)} %copy-done) | copy-start | bytes 4669444
  65.4 1.1 %copy-start.6 = (f32[3,256]{1,0:T(4,128)S(1)}, f32[3,256]{1,0:T(4,128)}, u32[]{:S(2)}) copy-start(f32[3,256]{1,0:T(4,128)} %obs_ref.1) | copy-start | bytes 9220
  65.4 1.1 %copy-start.9 = (f32[64]{0:T(128)S(1)}, f32[64]{0:T(128)}, u32[]{:S(2)}) copy-start(f32[64]{0:T(128)} %freq_ref.1) | copy-start | bytes 772

commit v2 on v1

--- a/solution.py
+++ b/solution.py
@@ -180,9 +180,19 @@
     return pltpu.roll(v, step % BZ, axis=1) if step else v
 
 
-def first_kernel(f_ref, solid_ref, relaxed_ref, up_ref, down_ref, moments_ref):
+def first_kernel(f_hbm, solid_hbm, relaxed_ref, up_ref, down_ref, moments_ref, f_ref, solid_ref, sems):
+    def plane(x):
+        return pltpu.make_async_copy(f_hbm.at[:, x], f_ref.at[:, x], sems.at[x])
+
+    mask = pltpu.make_async_copy(solid_hbm, solid_ref, sems.at[BX])
+    mask.start()
+    for x in range(BX):
+        plane(x).start()
+    mask.wait()
+
     @pl.loop(0, BX)
     def _(x):
+        plane(x).wait()
         for t in range(BY // 8):
             rows = pl.ds(t * 8, 8)
             f = [f_ref[i, x, rows, :] for i in range(NQ)]
@@ -268,7 +278,7 @@
 
 def steps_kernel(
     relaxed_ref, solid_ref, low_ref, high_ref, below_ref, above_ref, table_ref,
-    out_ref, up_ref, down_ref, message_ref, ext_a, ext_b, moments,
+    out_hbm, up_ref, down_ref, message_ref, ext_a, ext_b, moments, out_ref, sem,
 ):
     for x in range(BX):
         for pop in range(NQ):
@@ -296,12 +306,8 @@
                     f.append(source[i, x - cx, pl.ds(row - cy, 8), :])
                 solid = ext_a[SOLID, x, pl.ds(row, 8), :] > 0.0
                 out, *sums = collide(f, solid)
-                if target is not None:
-                    for i in range(NQ):
-                        target[i, x, pl.ds(row, 8), :] = turn(out[i], i)
-                else:
-                    for i in range(NQ):
-                        out_ref[i, x - HX, pl.ds(t * 8, 8), :] = turn(out[i], i)
+                for i in range(NQ):
+                    target[i, x, pl.ds(row, 8), :] = turn(out[i], i)
 
                 at = pl.ds(pl.multiple_of(x * (BY + 8) + t * 8, 8), 8)
                 for q, v in enumerate(sums):
@@ -313,16 +319,21 @@
 
     step(ext_a, ext_b, 2, 0)
     step(ext_b, ext_a, 1, 1)
-    step(ext_a, None, 0, 2)
+    step(ext_a, ext_b, 0, 2)
     n = 0
     m = 0
     for pop in range(NQ):
-        if VEL[pop][0] > 0:
-            up_ref[n] = out_ref[pop, BX - 1]
+        cx, cy, _ = VEL[pop]
+        if cx > 0:
+            up_ref[n] = ext_b[pop, HX + BX - 1, 8 : 48, :]
             n += 1
-        if VEL[pop][0] < 0:
-            down_ref[m] = out_ref[pop, 0]
+        if cx < 0:
+            down_ref[m] = ext_b[pop, HX, 8 : 48, :]
             m += 1
+        for x in range(max(cx, 0), BX + min(cx, 0)):
+            out_ref[pop, x] = ext_b[pop, x + HX - cx, Y0 - cy : Y0 - cy + BY, :]
+    result = pltpu.make_async_copy(out_ref, out_hbm, sem)
+    result.start()
     table = table_ref[...]
     columns = []
     for which in range(3):
@@ -330,25 +341,24 @@
         sums = [moments[which, q, inside, :] for q in range(4)]
         columns += sample(sums, table, 1, BX * (BY + 8))
     put_message(lanes_of(columns), message_ref)
-
-
-def last_kernel(relaxed_ref, low_ref, high_ref, out_ref):
-    n = 0
-    m = 0
-    for pop in range(NQ):
-        cx, cy, _ = VEL[pop]
-        for x in range(BX):
-            for t in range(BY // 8):
-                row = 4 + 8 * t - cy
-                if x - cx < 0:
-                    v = low_ref[n, row : row + 8, :]
-                elif x - cx >= BX:
-                    v = high_ref[m, row : row + 8, :]
-                else:
-                    v = relaxed_ref[pop, x - cx, row : row + 8, :]
-                out_ref[pop, x, t * 8 : t * 8 + 8, :] = v
-        n += cx > 0
-        m += cx < 0
+    result.wait()
+
+
+EDGES = [(pop, 0) for pop in range(NQ) if VEL[pop][0] > 0] + [
+    (pop, BX - 1) for pop in range(NQ) if VEL[pop][0] < 0
+]
+
+
+def last_kernel(given_ref, low_ref, high_ref, out_ref, planes, sems):
+    copies = []
+    for n, (pop, x) in enumerate(EDGES):
+        source = low_ref.at[n] if x == 0 else high_ref.at[n - 5]
+        row = 4 - VEL[pop][1]
+        planes[n] = source[row : row + BY, :]
+        copies.append(pltpu.make_async_copy(planes.at[n], out_ref.at[pop, x], sems.at[n]))
+        copies[-1].start()
+    for copy in copies:
+        copy.wait()
 
 
 def fit(fun, degree, odd):
@@ -388,10 +398,48 @@
 
 
 CHUNKS = NB * CAP // 128
-
-
-def sum_kernel(
-    freq_ref, first_ref, second_ref, obs_ref, out_ref, info, series, weights, acc, obs_lanes, places
+TILES = 2
+WIDE = 4
+AHEAD = 2
+
+
+def parts_of(message):
+    turned = message.T
+    return [jnp.concatenate(split3(turned[r * NV : r * NV + NV, :]), axis=0) for r in range(8)]
+
+
+def pack(parts, places, c):
+    lanes = lax.broadcasted_iota(jnp.int32, (2 * NB, 128), 1)
+    here = (lanes + c * 128).astype(F32)
+    total = jnp.zeros((3 * NV, 128), F32)
+    for r in range(8):
+        hot = jnp.where(places[r] == here, 1.0, 0.0).astype(BF16)
+        total = total + dot(parts[r], hot)
+    return total[:NV] + total[NV : 2 * NV] + total[2 * NV :]
+
+
+def distances(obs_lanes, info, c, rows):
+    d = [obs_lanes[k, rows, :] - info[c, k : k + 1, :] for k in range(3)]
+    square = d[0] * d[0] + d[1] * d[1] + d[2] * d[2]
+    inv = lax.rsqrt(square)
+    return d, inv, square * inv
+
+
+def tile_rows(o, t, tiles):
+    return pl.ds(pl.multiple_of(o * 8 * tiles + 8 * t, 8), 8)
+
+
+def fill_places(spots, places):
+    for r in range(8):
+        places[r] = jnp.where(spots[1] > float(r), spots[0] + float(r), -1.0)
+
+
+def count_of(total_ref):
+    return (jnp.sum(total_ref[0:1, 0:1]).astype(jnp.int32) + 127) // 128
+
+
+def table_kernel(
+    freq_ref, first_ref, obs_ref, waves_hbm, spots, info, obs_lanes, total_ref, places, waves, sems
 ):
     lane = lax.broadcasted_iota(jnp.int32, (2 * NB, 128), 1)
     first = first_ref[...]
@@ -402,31 +450,82 @@
     ).astype(F32).astype(BF16)
     live_lanes = jnp.broadcast_to(live, (2 * NB, 128))
     offset = dot(lower, live_lanes.astype(BF16))
-    total = jnp.sum(live).astype(jnp.int32)
-    chunks = (total + 127) // 128
-    for r in range(8):
-        places[r] = jnp.where(live_lanes > float(r), offset + float(r), -1.0)
-    turned = [first.T, second_ref[...].T]
-    parts = []
-    for r in range(8):
-        both = jnp.concatenate([v[r * NV : r * NV + NV, :] for v in turned], axis=0)
-        parts.append(jnp.concatenate(split3(both), axis=0))
-    lanes = lax.broadcasted_iota(jnp.int32, (2 * NB, 128), 1)
+    total = jnp.sum(live)
+    total_ref[...] = jnp.broadcast_to(jnp.sum(live, axis=0, keepdims=True), (8, 128))
+    chunks = (total.astype(jnp.int32) + 127) // 128
+    spots[0] = offset
+    spots[1] = live_lanes
+    fill_places(spots, places)
+    parts = parts_of(first)
+    observers = obs_ref[...]
+    for k in range(3):
+        obs_lanes[k] = jnp.broadcast_to(observers[k : k + 1, :], (128, 256)).T
+    gy = lax.axis_index("gy") * 8
+    turns = [freq_ref[gy + k] * (math.sqrt(3.0) / (2.0 * math.pi)) for k in range(AHEAD)]
+
+    def store(c):
+        slot = c % 2
+        return pltpu.make_async_copy(waves.at[slot], waves_hbm.at[c], sems.at[slot])
 
     @pl.loop(0, chunks)
     def _(c):
-        here = (lanes + c * 128).astype(F32)
-        packed = jnp.zeros((6 * NV, 128), F32)
-        for r in range(8):
-            hot = jnp.where(places[r] == here, 1.0, 0.0).astype(BF16)
-            packed = packed + dot(parts[r], hot)
-        value = packed[: 2 * NV] + packed[2 * NV : 4 * NV] + packed[4 * NV :]
-        info[c] = value[0:8, :]
-        area = [value[4 + k : 5 + k, :] for k in range(3)]
-        keep = value[3:4, :]
+        info[c] = pack(parts, places, c)
+        slot = c % 2
+
+        @pl.when(c >= 2)
+        def _():
+            store(c - 2).wait()
+
+        @pl.loop(0, 32 // WIDE)
+        def _(o):
+            tiles = []
+            for t in range(WIDE):
+                rows = tile_rows(o, t, WIDE)
+                _, inv, dist = distances(obs_lanes, info, c, rows)
+                tiles.append((rows, inv, dist))
+            for k in range(AHEAD):
+                for rows, inv, dist in tiles:
+                    cos, sin = sin_cos_turns(dist * turns[k])
+                    waves[slot, 2 * k, rows, :] = cos * inv
+                    waves[slot, 2 * k + 1, rows, :] = sin * inv
+
+        store(c).start()
+
+    @pl.when(chunks >= 2)
+    def _():
+        store(chunks - 2).wait()
+
+    store(chunks - 1).wait()
+
+
+def sum_kernel(
+    freq_ref, waves_hbm, second_ref, spots, info, obs_lanes, total_ref, out_ref,
+    series, weights, acc, places, waves, sems,
+):
+    chunks = count_of(total_ref)
+
+    def load(c):
+        slot = c % 2
+        return pltpu.make_async_copy(waves_hbm.at[c], waves.at[slot], sems.at[slot])
+
+    load(0).start()
+
+    @pl.when(chunks >= 2)
+    def _():
+        load(1).start()
+
+    fill_places(spots, places)
+    parts = parts_of(second_ref[...])
+
+    @pl.loop(0, chunks)
+    def _(c):
+        late = pack(parts, places, c)
+        fixed = info[c]
+        area = [fixed[4 + k : 5 + k, :] for k in range(3)]
+        keep = fixed[3:4, :]
         rows = []
         for s in range(4):
-            at = 7 if s == 0 else 2 * NV // 2 + 4 * (s - 1)
+            value, at = (fixed, 7) if s == 0 else (late, 4 * (s - 1))
             rho = value[at : at + 1, :]
             j = [value[at + 1 + k : at + 2 + k, :] for k in range(3)]
             scale = 1.0 / jnp.where(keep > 0.0, rho, 1.0)
@@ -460,44 +559,44 @@
                     v = v * (1.0 / math.sqrt(3.0))
                 weights[c, part * 4 + comp] = v
 
-    observers = obs_ref[...]
-    for k in range(3):
-        obs_lanes[k] = jnp.broadcast_to(observers[k : k + 1, :], (128, 256)).T
-
     turns = [freq_ref[gy + k] * (math.sqrt(3.0) / (2.0 * math.pi)) for k in range(8)]
     over_k = [1.0 / (omega[k : k + 1, :] * math.sqrt(3.0)) for k in range(8)]
     over_k = [jnp.broadcast_to(v, (8, 128)) for v in over_k]
-
-    @pl.loop(0, 32)
-    def _(o):
-        rows = pl.ds(pl.multiple_of(o * 8, 8), 8)
-        place = [obs_lanes[k, rows, :] for k in range(3)]
-
-        def body(c, carry):
-            d = [place[k] - info[c, k : k + 1, :] for k in range(3)]
-            square = d[0] * d[0] + d[1] * d[1] + d[2] * d[2]
-            inv = lax.rsqrt(square)
-            dist = square * inv
-            n = [v * inv for v in d]
-            out = []
+    acc[...] = jnp.zeros_like(acc)
+
+    @pl.loop(0, chunks)
+    def _(c):
+        slot = c % 2
+        load(c).wait()
+
+        @pl.loop(0, 32 // TILES)
+        def _(o):
+            tiles = []
+            for t in range(TILES):
+                rows = tile_rows(o, t, TILES)
+                d, inv, dist = distances(obs_lanes, info, c, rows)
+                tiles.append((rows, inv, dist, [v * inv for v in d]))
             for k in range(8):
-                cos, sin = sin_cos_turns(dist * turns[k])
                 w = [weights[c, m, k : k + 1, :] for m in range(8)]
-                re = n[0] * w[1] + n[1] * w[2] + n[2] * w[3]
-                im = n[0] * w[5] + n[1] * w[6] + n[2] * w[7]
-                near = inv * over_k[k]
-                dr = near * re - (im + w[4])
-                di = near * im + (re + w[0])
-                cos = cos * inv
-                sin = sin * inv
-                out.append(carry[2 * k] + (cos * dr + sin * di))
-                out.append(carry[2 * k + 1] + (cos * di - sin * dr))
-            return tuple(out)
-
-        sums = lax.fori_loop(0, chunks, body, tuple(jnp.zeros((8, 128), F32) for _ in range(16)))
-        for k in range(8):
-            acc[k, rows, :] = sums[2 * k]
-            acc[8 + k, rows, :] = sums[2 * k + 1]
+                for rows, inv, dist, n in tiles:
+                    if k < AHEAD:
+                        cos = waves[slot, 2 * k, rows, :]
+                        sin = waves[slot, 2 * k + 1, rows, :]
+                    else:
+                        cos, sin = sin_cos_turns(dist * turns[k])
+                        cos = cos * inv
+                        sin = sin * inv
+                    re = n[0] * w[1] + n[1] * w[2] + n[2] * w[3]
+                    im = n[0] * w[5] + n[1] * w[6] + n[2] * w[7]
+                    near = inv * over_k[k]
+                    dr = near * re - (im + w[4])
+                    di = near * im + (re + w[0])
+                    acc[k, rows, :] += cos * dr + sin * di
+                    acc[8 + k, rows, :] += cos * di - sin * dr
+
+        @pl.when(c + 2 < chunks)
+        def _():
+            load(c + 2).start()
 
     ones = jnp.ones((8, 128), BF16)
     for k in range(16):
@@ -510,17 +609,29 @@
         out_ref[k // 8, k % 8 : k % 8 + 1, :] = whole[0:1, :] * wave
 
 
-def call(kernel, shapes, scratch=(), smem=0, inputs=0, cost=1000, limit=8):
+def call(
+    kernel, shapes, scratch=(), smem=0, inputs=0, cost=1000, limit=8, far=0, alias=None, out_far=0
+):
+    near = pl.BlockSpec(memory_space=pltpu.VMEM)
     return pl.pallas_call(
         kernel,
-        out_shape=[jax.ShapeDtypeStruct(s, F32) for s in shapes],
+        out_shape=[
+            pltpu.HBM(s, F32) if n < out_far else jax.ShapeDtypeStruct(s, F32)
+            for n, s in enumerate(shapes)
+        ],
         in_specs=[pl.BlockSpec(memory_space=pltpu.SMEM)] * smem
-        + [pl.BlockSpec(memory_space=pltpu.VMEM)] * (inputs - smem),
-        out_specs=[pl.BlockSpec(memory_space=pltpu.VMEM)] * len(shapes),
+        + [pl.BlockSpec(memory_space=pltpu.HBM)] * far
+        + [near] * (inputs - smem - far),
+        out_specs=[pl.BlockSpec(memory_space=pltpu.HBM)] * out_far + [near] * (len(shapes) - out_far),
         scratch_shapes=list(scratch),
+        input_output_aliases=alias or {},
         compiler_params=pltpu.CompilerParams(vmem_limit_bytes=limit << 20),
         cost_estimate=pl.CostEstimate(flops=cost, bytes_accessed=cost, transcendentals=0),
     )
+
+
+def far_away(array):
+    return pltpu.with_memory_space_constraint(array, pltpu.HBM)
 
 
 def ring(axis, up, down):
@@ -544,9 +655,15 @@
     relaxed, up, down, moments = call(
         first_kernel,
         [(NQ, BX, BY, BZ), (NXE, BY, BZ), (NXE, BY, BZ), (4, BX * BY, BZ)],
+        [
+            pltpu.VMEM((NQ, BX, BY, BZ), F32),
+            pltpu.VMEM((BX, BY, BZ), jnp.int32),
+            pltpu.SemaphoreType.DMA((BX + 1,)),
+        ],
         inputs=2,
+        far=2,
         limit=12,
-    )(populations, solid)
+    )(far_away(populations), far_away(solid))
     table, message_a = call(
         slots_kernel, [(SLOTS, 128), (2 * NB, 128)], smem=1, inputs=5
     )(panel_count, cell, owner, panel_area, moments)
@@ -554,35 +671,67 @@
     y_up, y_down = call(edge_kernel, [(NYE, BZ)] * 2, inputs=4)(relaxed, solid, low, high)
     below, above = ring("gy", y_up, y_down)
     got_a = exchange(message_a)
-    relaxed, up, down, message_b = call(
+    current, up, down, message_b = call(
         steps_kernel,
-        [(NQ, BX, BY + 8, BZ), (5, BY + 8, BZ), (5, BY + 8, BZ), (2 * NB, 128)],
+        [(NQ, BX, BY, BZ), (5, BY + 8, BZ), (5, BY + 8, BZ), (2 * NB, 128)],
         [
             pltpu.VMEM((NQ + 1, BX + 2 * HX, YR, BZ), F32),
             pltpu.VMEM((NQ, BX + 2 * HX, YR, BZ), F32),
             pltpu.VMEM((3, 4, (BX + 2 * HX) * (BY + 8), BZ), F32),
+            pltpu.VMEM((NQ, BX, BY, BZ), F32),
+            pltpu.SemaphoreType.DMA,
         ],
+        out_far=1,
         inputs=7,
         limit=28,
     )(relaxed, solid, low, high, below, above, table)
     got_b = exchange(message_b)
     low, high = ring("gx", up, down)
-    (current,) = call(last_kernel, [(NQ, BX, BY, BZ)], inputs=3)(relaxed, low, high)
+    (current,) = call(
+        last_kernel,
+        [(NQ, BX, BY, BZ)],
+        [pltpu.VMEM((len(EDGES), BY, BZ), F32), pltpu.SemaphoreType.DMA((len(EDGES),))],
+        inputs=3,
+        far=1,
+        out_far=1,
+        alias={0: 0},
+        limit=4,
+    )(current, low, high)
+    waves, *tables = call(
+        table_kernel,
+        [
+            (CHUNKS, 2 * AHEAD, 256, 128),
+            (2, 2 * NB, 128),
+            (CHUNKS, NV, 128),
+            (3, 256, 128),
+            (8, 128),
+        ],
+        [
+            pltpu.VMEM((8, 2 * NB, 128), F32),
+            pltpu.VMEM((2, 2 * AHEAD, 256, 128), F32),
+            pltpu.SemaphoreType.DMA((2,)),
+        ],
+        out_far=1,
+        smem=1,
+        inputs=3,
+        limit=6,
+    )(frequencies, got_a, observers)
     (spectra,) = call(
         sum_kernel,
         [(2, 8, 256)],
         [
-            pltpu.VMEM((CHUNKS, 8, 128), F32),
             pltpu.VMEM((CHUNKS, 16, 128), F32),
             pltpu.VMEM((CHUNKS, 8, 8, 128), F32),
             pltpu.VMEM((16, 256, 128), F32),
-            pltpu.VMEM((3, 256, 128), F32),
             pltpu.VMEM((8, 2 * NB, 128), F32),
+            pltpu.VMEM((2, 2 * AHEAD, 256, 128), F32),
+            pltpu.SemaphoreType.DMA((2,)),
         ],
         smem=1,
-        inputs=4,
-        limit=14,
-    )(frequencies, got_a, got_b, observers)
+        far=1,
+        inputs=7,
+        limit=10,
+    )(frequencies, far_away(waves), got_b, *tables)
     return current, spectra[None]
 
 

time: 95.2 us -> 89.7 us (0.942)
  local copies, waits for them, and re-layouts: 5.35 us -> 0.67 us
  waiting for transfers between devices: 16.7 us -> 13.8 us
  Pallas kernels: 39.6 us -> 41.8 us
    unnamed x22 -> x14, local copies, waits for them, and re-layouts: 5.35 us -> 0.67 us
    ppermute x3, waiting for transfers between devices: 15.6 us -> 12.6 us  [ring(): low = lax.ppermute(up, axis, forward)]
    pallas_call x3 -> x4, Pallas kernels: 36.1 us -> 37.2 us  [the longest x1 21.7 us: run(): call(sum_kernel, [(2, 8, 256)], [pltpu.VMEM((CHUNKS, 16, 128), F32), pltp...]
    pallas_call x1, Pallas kernels: 0.86 us -> 1.95 us  [run(): call(first_kernel, [(NQ, BX, BY, BZ), (NXE, BY, BZ), (NXE, BY, BZ), (4, B...]
  transfers between devices with their start and end apart: 8 -> 8, of which waited for: 3 -> 2; matrix products, arithmetic and copies ran while one was open for 0% -> 0% of each run, Pallas kernels for 10% -> 19%
where the time goes in v2:
time: 89.7 us; the launch traced here: 89.5 us
  Pallas kernels  41.8 us (47%)
  starting transfers between devices  31.8 us (35%)
  waiting for transfers between devices  13.8 us (15%)
  between operations  1.46 us (2%)
    pallas_call x1, Pallas kernels, run(): call(sum_kernel, [(2, 8, 256)], [pltpu.VMEM((CHUNKS, 16, 128), F32), pltp...  21.7 us
    all_to_all x2, starting transfers between devices, exchange(): lax.all_to_all(message, ('gx', 'gy'), split_axis=0, concat_axis=0, tiled=...  17.6 us
    ppermute x3, waiting for transfers between devices, ring(): low = lax.ppermute(up, axis, forward)  12.6 us
    ppermute x3, starting transfers between devices, ring(): high = lax.ppermute(down, axis, backward)  12.5 us
    pallas_call x1, Pallas kernels, run(): call(steps_kernel, [(NQ, BX, BY, BZ), (5, BY + 8, BZ), (5, BY + 8, BZ), (...  7.61 us
    pallas_call x1, Pallas kernels, run(): call(table_kernel, [(CHUNKS, 2 * AHEAD, 256, 128), (2, 2 * NB, 128), (CHU...  7.18 us
    pallas_call x1, Pallas kernels, run(): call(first_kernel, [(NQ, BX, BY, BZ), (NXE, BY, BZ), (NXE, BY, BZ), (4, B...  1.95 us
  transfers between devices with their start and end apart: 8, of which 2 were waited for; matrix products, arithmetic and copies ran while one was open for 0% of the time, Pallas kernels for 19%

profile of v2, /device:TPU:0, one launch (start us, length us, event | category | flops | bytes accessed | tf_op | source)
XLA Modules:
  0.0 89.5 jit_solution(11529716705226641967)
XLA Ops:
  0.6 0.0 copy-start
  0.6 2.0 %shard_map.95 = (f32[19,4,32,128]{3,2,1,0:T(8,128)S(1)}, f32[40,32,128]{2,1,0:T(8,128)S(1)}, f32[40,32,128]{2,1,0:T(8,128)S(1)}, f32[4,128,128]{2,1,0:T(8,128)S(1)}) custom-call(f32[19,4,32,128]{3,2,1,0:T(8,128)} %f_hbm.1, s32[4,32,128]{2,1,0:T(8,128)} %solid_ref.3), custom_call_target="tpu_custom_call" | custom-call | flops 1000 | bytes 1000 | tf_op jit(solution)/shard_map/pallas_call | solution.py:655
  2.6 0.1 collective-permute-start
  2.7 4.6 %collective-permute-start.1 = (f32[40,32,128]{2,1,0:T(8,128)S(1)}, f32[40,32,128]{2,1,0:T(8,128)S(1)}, u32[]{:S(2)}, u32[]{:S(2)}) collective-permute-start(f32[40,32,128]{2,1,0:T(8,128)S(1)} %get-tuple-element.21), channel_id=1, source_target_pairs={{8,0},{16,8},{24,16},{32,24},{40,32},{48,40},{56,48},{64,56},{72,6... | collective-permute-start | bytes 1966088 | tf_op jit(solution)/shard_map/ppermute | solution.py:642
  7.3 12.6 %collective-permute-done.low_ref = f32[40,32,128]{2,1,0:T(8,128)S(1)} collective-permute-done((f32[40,32,128]{2,1,0:T(8,128)S(1)}, f32[40,32,128]{2,1,0:T(8,128)S(1)}, u32[]{:S(2)}, u32[]{:S(2)}) %collective-permute-start) | collective-permute-done | bytes 655392 | tf_op jit(solution)/shard_map/ppermute | solution.py:641
  19.9 0.0 collective-permute-done.1.high_ref
  19.9 0.0 copy-done
  19.9 0.0 copy-start.1
  19.9 0.0 copy-start.4
  19.9 0.0 copy-start.5
  19.9 0.9 %shard_map.96 = (f32[480,128]{1,0:T(8,128)}, f32[480,128]{1,0:T(8,128)}) custom-call(f32[19,4,32,128]{3,2,1,0:T(8,128)S(1)} %get-tuple-element.19.relaxed_ref, s32[4,32,128]{2,1,0:T(8,128)S(1)} %copy-done, f32[40,32,128]{2,1,0:T(8,128)S(1)} %collective-permute-done.low_ref, f32[40,32,128]{2,1,0:T(8,128)S(1)} %collective-permute-done.1.high_ref), custom_call_target="tpu_custom_call" | custom-call | flops 1000 | bytes 1000 | tf_op jit(solution)/shard_map/pallas_call | solution.py:671
  20.8 1.6 %collective-permute-start.2 = (f32[480,128]{1,0:T(8,128)}, f32[480,128]{1,0:T(8,128)S(1)}, u32[]{:S(2)}, u32[]{:S(2)}) collective-permute-start(f32[480,128]{1,0:T(8,128)} %get-tuple-element.22), channel_id=1, source_target_pairs={{0,1},{1,2},{2,3},{3,4},{4,5},{5,6},{6,7},{7,0},{8,9},{9,10},{10,1... | collective-permute-start | bytes 737288 | tf_op jit(solution)/shard_map/ppermute | solution.py:641
  22.4 4.1 %collective-permute-start.3 = (f32[480,128]{1,0:T(8,128)}, f32[480,128]{1,0:T(8,128)S(1)}, u32[]{:S(2)}, u32[]{:S(2)}) collective-permute-start(f32[480,128]{1,0:T(8,128)} %get-tuple-element.23), channel_id=1, source_target_pairs={{1,0},{2,1},{3,2},{4,3},{5,4},{6,5},{7,6},{0,7},{9,8},{10,9},{11,1... | collective-permute-start | bytes 737288 | tf_op jit(solution)/shard_map/ppermute | solution.py:642
  27.1 0.0 copy-done.1
  27.1 0.0 copy-done.4
  27.2 0.0 copy-done.5
  27.2 1.7 %shard_map.97 = (f32[256,128]{1,0:T(8,128)S(1)}, f32[256,128]{1,0:T(8,128)}) custom-call(s32[1]{0:T(128)S(6)} %copy.12.count_ref, s32[1,256]{1,0:T(1,128)S(1)} %bitcast.9, s32[1,256]{1,0:T(1,128)S(1)} %bitcast.10, f32[3,256]{1,0:T(4,128)S(1)} %copy-done.1, f32[4,128,128]{2,1,0:T(8,128)S(1)} %get-tuple-element.24.moments_ref), custom_call_target="tpu_custom_call" | custom-call | flops 1000 | bytes 1000 | tf_op jit(solution)/shard_map/pallas_call | solution.py:667
  28.9 9.0 %all-to-all-start = ((f32[128,2,128]{2,1,0:T(2,128)}), f32[128,2,128]{2,1,0:T(2,128)S(1)}, u32[]{:S(2)}, u32[]{:S(2)}) async-start(f32[128,2,128]{2,1,0:T(2,128)} %bitcast.2), calls=%async_computation | async-start | bytes 262144 | tf_op jit(solution)/shard_map/all_to_all | solution.py:647
  37.8 0.0 collective-permute-done.2.below_ref
  37.8 0.0 collective-permute-done.3.above_ref
  37.9 0.0 copy-start.2
  37.9 0.0 copy-start.3
  37.9 7.6 %shard_map.98 = (f32[19,4,32,128]{3,2,1,0:T(8,128)}, f32[5,40,128]{2,1,0:T(8,128)S(1)}, f32[5,40,128]{2,1,0:T(8,128)S(1)}, f32[256,128]{1,0:T(8,128)}) custom-call(f32[19,4,32,128]{3,2,1,0:T(8,128)S(1)} %get-tuple-element.19.relaxed_ref, s32[4,32,128]{2,1,0:T(8,128)S(1)} %copy-done, f32[40,32,128]{2,1,0:T(8,128)S(1)} %collective-permute-done.low_ref, ...), custom_call_target="tpu_custom_call" | custom-call | flops 1000 | bytes 1000 | tf_op jit(solution)/shard_map/pallas_call | solution.py:674
  45.5 0.0 copy-start.6
  45.5 0.6 copy-done.6
  46.1 1.1 %all-to-all-done = f32[128,2,128]{2,1,0:T(2,128)S(1)} async-done(((f32[128,2,128]{2,1,0:T(2,128)}), f32[128,2,128]{2,1,0:T(2,128)S(1)}, u32[]{:S(2)}, u32[]{:S(2)}) %all-to-all-start) | async-done | bytes 131104 | tf_op jit(solution)/shard_map/all_to_all | solution.py:647
  47.3 8.6 %all-to-all-start.1 = ((f32[128,2,128]{2,1,0:T(2,128)}), f32[128,2,128]{2,1,0:T(2,128)S(1)}, u32[]{:S(2)}, u32[]{:S(2)}) async-start(f32[128,2,128]{2,1,0:T(2,128)} %bitcast.4), calls=%async_computation.1 | async-start | bytes 262144 | tf_op jit(solution)/shard_map/all_to_all | solution.py:647
  55.9 0.1 collective-permute-start.4
  56.0 3.8 %collective-permute-start.5 = (f32[5,40,128]{2,1,0:T(8,128)S(1)}, f32[5,40,128]{2,1,0:T(8,128)S(1)}, u32[]{:S(2)}, u32[]{:S(2)}) collective-permute-start(f32[5,40,128]{2,1,0:T(8,128)S(1)} %get-tuple-element.28), channel_id=1, source_target_pairs={{8,0},{16,8},{24,16},{32,24},{40,32},{48,40},{56,48},{64,56},{72,6... | collective-permute-start | bytes 307208 | tf_op jit(solution)/shard_map/ppermute | solution.py:642
  59.8 0.0 copy-done.2
  59.9 0.0 copy-done.3
  59.9 7.2 %shard_map.100 = (f32[16,4,256,128]{3,2,1,0:T(8,128)}, f32[2,256,128]{2,1,0:T(8,128)S(1)}, f32[16,16,128]{2,1,0:T(8,128)S(1)}, f32[3,256,128]{2,1,0:T(8,128)S(1)}, f32[8,128]{1,0:T(8,128)S(1)}) custom-call(f32[64]{0:T(128)S(1)} %copy-done.3, f32[256,128]{1,0:T(8,128)S(1)} %bitcast.8, f32[3,256]{1,0:T(4,128)S(1)} %copy-done.2), custom_call_target="tpu_custom_call" | custom-call | flops 1000 | bytes 1000 | tf_op jit(solution)/shard_map/pallas_call | solution.py:700
  67.0 0.0 collective-permute-done.4.low_ref
  67.0 0.0 collective-permute-done.5.high_ref
  67.1 0.7 shard_map.99
  67.8 0.0 all-to-all-done.1
  67.8 21.7 %shard_map.101 = f32[2,8,256]{2,1,0:T(8,128)} custom-call(f32[64]{0:T(128)S(1)} %copy-done.3, f32[16,4,256,128]{3,2,1,0:T(8,128)} %get-tuple-element.30.waves_hbm, f32[256,128]{1,0:T(8,128)S(1)} %bitcast.7, f32[2,256,128]{2,1,0:T(8,128)S(1)} %get-tuple-element.32.spots, f32[16,16,128]{2,1,0:T(8,128)S(1)} %get-tuple-element.33.info, ...), custom_call_target="tpu_custom_call" | custom-call | flops 1000 | bytes 1000 | tf_op jit(solution)/shard_map/pallas_call | solution.py:719
Async XLA Ops:
  0.6 19.3 %copy-start = (s32[4,32,128]{2,1,0:T(8,128)S(1)}, s32[4,32,128]{2,1,0:T(8,128)}, u32[]{:S(2)}) copy-start(s32[4,32,128]{2,1,0:T(8,128)} %solid_ref.3) | copy-start | bytes 196612
  2.6 17.3 %collective-permute-start = (f32[40,32,128]{2,1,0:T(8,128)S(1)}, f32[40,32,128]{2,1,0:T(8,128)S(1)}, u32[]{:S(2)}, u32[]{:S(2)}) collective-permute-start(f32[40,32,128]{2,1,0:T(8,128)S(1)} %get-tuple-element.20), channel_id=1, source_target_pairs={{0,8},{8,16},{16,24},{24,32},{32,40},{40,48},{48,56},{56,64},{64,7... | collective-permute-start | bytes 1966088 | tf_op jit(solution)/shard_map/ppermute | solution.py:641
  2.7 17.2 %collective-permute-start.1 = (f32[40,32,128]{2,1,0:T(8,128)S(1)}, f32[40,32,128]{2,1,0:T(8,128)S(1)}, u32[]{:S(2)}, u32[]{:S(2)}) collective-permute-start(f32[40,32,128]{2,1,0:T(8,128)S(1)} %get-tuple-element.21), channel_id=1, source_target_pairs={{8,0},{16,8},{24,16},{32,24},{40,32},{48,40},{56,48},{64,56},{72,6... | collective-permute-start | bytes 1966088 | tf_op jit(solution)/shard_map/ppermute | solution.py:642
  19.9 7.3 %copy-start.1 = (f32[3,256]{1,0:T(4,128)S(1)}, f32[3,256]{1,0:T(4,128)}, u32[]{:S(2)}) copy-start(f32[3,256]{1,0:T(4,128)} %area_ref.1) | copy-start | bytes 9220
  19.9 7.3 %copy-start.4 = (s32[256]{0:T(256)S(1)}, s32[256]{0:T(256)}, u32[]{:S(2)}) copy-start(s32[256]{0:T(256)} %param.10) | copy-start | bytes 3076
  19.9 7.3 %copy-start.5 = (s32[256]{0:T(256)S(1)}, s32[256]{0:T(256)}, u32[]{:S(2)}) copy-start(s32[256]{0:T(256)} %param.11) | copy-start | bytes 3076
  20.8 17.0 %collective-permute-start.2 = (f32[480,128]{1,0:T(8,128)}, f32[480,128]{1,0:T(8,128)S(1)}, u32[]{:S(2)}, u32[]{:S(2)}) collective-permute-start(f32[480,128]{1,0:T(8,128)} %get-tuple-element.22), channel_id=1, source_target_pairs={{0,1},{1,2},{2,3},{3,4},{4,5},{5,6},{6,7},{7,0},{8,9},{9,10},{10,1... | collective-permute-start | bytes 737288 | tf_op jit(solution)/shard_map/ppermute | solution.py:641
  22.4 15.4 %collective-permute-start.3 = (f32[480,128]{1,0:T(8,128)}, f32[480,128]{1,0:T(8,128)S(1)}, u32[]{:S(2)}, u32[]{:S(2)}) collective-permute-start(f32[480,128]{1,0:T(8,128)} %get-tuple-element.23), channel_id=1, source_target_pairs={{1,0},{2,1},{3,2},{4,3},{5,4},{6,5},{7,6},{0,7},{9,8},{10,9},{11,1... | collective-permute-start | bytes 737288 | tf_op jit(solution)/shard_map/ppermute | solution.py:642
  28.9 18.4 %all-to-all-start = ((f32[128,2,128]{2,1,0:T(2,128)}), f32[128,2,128]{2,1,0:T(2,128)S(1)}, u32[]{:S(2)}, u32[]{:S(2)}) async-start(f32[128,2,128]{2,1,0:T(2,128)} %bitcast.2), calls=%async_computation | async-start | bytes 262144 | tf_op jit(solution)/shard_map/all_to_all | solution.py:647
  37.9 22.0 %copy-start.2 = (f32[3,256]{1,0:T(4,128)S(1)}, f32[3,256]{1,0:T(4,128)}, u32[]{:S(2)}) copy-start(f32[3,256]{1,0:T(4,128)} %obs_ref.1) | copy-start | bytes 9220
  37.9 22.0 %copy-start.3 = (f32[64]{0:T(128)S(1)}, f32[64]{0:T(128)}, u32[]{:S(2)}) copy-start(f32[64]{0:T(128)} %freq_ref.3) | copy-start | bytes 772
  45.5 0.6 copy-start.6
  47.3 20.5 %all-to-all-start.1 = ((f32[128,2,128]{2,1,0:T(2,128)}), f32[128,2,128]{2,1,0:T(2,128)S(1)}, u32[]{:S(2)}, u32[]{:S(2)}) async-start(f32[128,2,128]{2,1,0:T(2,128)} %bitcast.4), calls=%async_computation.1 | async-start | bytes 262144 | tf_op jit(solution)/shard_map/all_to_all | solution.py:647
  55.9 11.1 %collective-permute-start.4 = (f32[5,40,128]{2,1,0:T(8,128)}, f32[5,40,128]{2,1,0:T(8,128)S(1)}, u32[]{:S(2)}, u32[]{:S(2)}) collective-permute-start(f32[5,40,128]{2,1,0:T(8,128)} %copy-done.6), channel_id=1, source_target_pairs={{0,8},{8,16},{16,24},{24,32},{32,40},{40,48},{48,56},{56,64},{64,7... | collective-permute-start | bytes 307208 | tf_op jit(solution)/shard_map/ppermute | solution.py:641
  56.0 11.0 %collective-permute-start.5 = (f32[5,40,128]{2,1,0:T(8,128)S(1)}, f32[5,40,128]{2,1,0:T(8,128)S(1)}, u32[]{:S(2)}, u32[]{:S(2)}) collective-permute-start(f32[5,40,128]{2,1,0:T(8,128)S(1)} %get-tuple-element.28), channel_id=1, source_target_pairs={{8,0},{16,8},{24,16},{32,24},{40,32},{48,40},{56,48},{64,56},{72,6... | collective-permute-start | bytes 307208 | tf_op jit(solution)/shard_map/ppermute | solution.py:642
